TPU v7x, 32 devices: a whole 2x2x4 slice. The times are simulated.
32 devices in a mesh: dp: 8 (over z, y), tensor: 4 (over x, core).
Axes of the slice: x: 2, y: 2, z: 4, core: 2. Of those that a mesh axis runs over, the one named last changes fastest.
Arguments:
- tokens: bfloat16 [8, 1024, 2048], P('dp'), may hold values from -6 to 6
- segment_ids: int32 [8, 1024], P('dp'), may hold values from 0 to 7, never falling along the last dimension, each value on 1 to 512 neighbouring positions
- out_grad: bfloat16 [8, 1024, 2048], P('dp'), may hold values from -6 to 6
- attn_norm_gain: float32 [2048], replicated, may hold values from 0.5 to 1.5
- attn_norm_bias: float32 [2048], replicated, may hold values from -1.75 to 1.75
- mlp_norm_gain: float32 [2048], replicated, may hold values from 0.5 to 1.5
- mlp_norm_bias: float32 [2048], replicated, may hold values from -1.75 to 1.75
- qkv_weight: float32 [2048, 8, 3, 256], P('dp', 'tensor'), may hold values from -0.1875 to 0.1875
- qv_bias: float32 [8, 2, 256], P('tensor'), may hold values from -1.75 to 1.75
- key_bias: float32 [8, 64], P('tensor'), may hold values from -3 to 3
- dense_weight: float32 [8, 256, 2048], P('tensor', None, 'dp'), may hold values from -0.75 to 0.75
- dense_bias: float32 [2048], replicated, may hold values from -1.75 to 1.75
- up_weight: float32 [2048, 8192], P('dp', 'tensor'), may hold values from -0.125 to 0.125
- up_bias: float32 [8192], P('tensor'), may hold values from -3 to 3
- down_weight: float32 [8192, 2048], P('tensor', 'dp'), may hold values from -0.0625 to 0.0625
- down_bias: float32 [2048], replicated, may hold values from -1.75 to 1.75
Outputs:
- block_out: bfloat16 [8, 1024, 2048], P('dp')
- input_grad: bfloat16 [8, 1024, 2048], P('dp')
- attn_norm_gain_grad: float32 [2048], replicated
- attn_norm_bias_grad: float32 [2048], replicated
- mlp_norm_gain_grad: float32 [2048], replicated
- mlp_norm_bias_grad: float32 [2048], replicated
- qkv_weight_grad: float32 [2048, 8, 3, 256], P('dp', 'tensor')
- qv_bias_grad: float32 [8, 2, 256], P('tensor')
- key_bias_grad: float32 [8, 64], P('tensor')
- dense_weight_grad: float32 [8, 256, 2048], P('tensor', None, 'dp')
- dense_bias_grad: float32 [2048], replicated
- up_weight_grad: float32 [2048, 8192], P('dp', 'tensor')
- up_bias_grad: float32 [8192], P('tensor')
- down_weight_grad: float32 [8192, 2048], P('tensor', 'dp')
- down_bias_grad: float32 [2048], replicated
Inputs may be any that keep to these rules, and one draw needn't show every extreme that they name: `segment_ids`: ids never fall along a sequence; each of the 8 documents of a sequence holds 1 to 512 tokens, one exactly 512.
All inputs are finite; a program needn't handle non-finite values.
Results may differ from a plain program's by a relative error of at most 0.007.
The roundings to bfloat16 on the way count: a program that leaves them out, or rounds other values in their place, can miss the bound.
Values may be sent and summed in bfloat16 or wider, within the bound.
A program may use at most 256 MiB of HBM per device.

v0:
```python
import jax
import jax.numpy as jnp
from jax import lax
from jax.sharding import PartitionSpec as P

ROT = 64
QBLOCK = 512


def norm_parts(values, gain_vec, offset):
    center = values - jnp.mean(values, axis=-1, keepdims=True)
    inverse = lax.rsqrt(jnp.mean(center * center, axis=-1, keepdims=True) + 1e-05)
    normed = center * inverse
    return (normed * gain_vec + offset, normed, inverse)


def norm_back(grad_out, normed, inverse, gain_vec):
    scaled = grad_out * gain_vec
    inner = (
        scaled
        - jnp.mean(scaled, axis=-1, keepdims=True)
        - normed * jnp.mean(scaled * normed, axis=-1, keepdims=True)
    )
    return (inner * inverse, jnp.sum(grad_out * normed, axis=0), jnp.sum(grad_out, axis=0))


def gelu_slope(pre_act):
    cumulative = 0.5 * (1.0 + lax.erf(pre_act * 0.7071067811865476))
    density = jnp.exp(-0.5 * pre_act * pre_act) * 0.3989422804014327
    return cumulative + pre_act * density


def rope_tables(length):
    half_rot = ROT // 2
    frequency = 10000.0 ** (-(jnp.arange(half_rot, dtype=jnp.float32) * 2.0) / ROT)
    angles = jnp.arange(length, dtype=jnp.float32)[:, None] * frequency[None, :]
    cosine = jnp.concatenate([jnp.cos(angles), jnp.cos(angles)], axis=-1)[:, None, :]
    sine_table = jnp.concatenate([jnp.sin(angles), jnp.sin(angles)], axis=-1)[:, None, :]
    return (cosine, sine_table)


def rotate(tensor, cosine, sine_table):
    half_rot = ROT // 2
    rotary_part = tensor[..., :ROT]
    turned = jnp.concatenate([-rotary_part[..., half_rot:], rotary_part[..., :half_rot]], axis=-1)
    return jnp.concatenate([rotary_part * cosine + turned * sine_table, tensor[..., ROT:]], axis=-1)


def body(
    tokens,
    segment_ids,
    out_grad,
    attn_norm_gain,
    attn_norm_bias,
    mlp_norm_gain,
    mlp_norm_bias,
    qkv_weight,
    qv_bias,
    key_bias,
    dense_weight,
    dense_bias,
    up_weight,
    up_bias,
    down_weight,
    down_bias,
):
    seq_count, length, model_width = tokens.shape
    row_count = seq_count * length
    heads_here = qkv_weight.shape[1]
    head_size = qkv_weight.shape[3]
    blocks = length // QBLOCK
    block_count = seq_count * blocks
    score_scale = head_size ** (-0.5)
    f_type = jnp.float32
    b_type = jnp.bfloat16
    inputs = tokens.reshape(row_count, model_width).astype(f_type)
    attn_in, attn_hat, attn_inv = norm_parts(inputs, attn_norm_gain, attn_norm_bias)
    mlp_in, mlp_hat, mlp_inv = norm_parts(inputs, mlp_norm_gain, mlp_norm_bias)
    attn_in = attn_in.astype(b_type)
    mlp_in = mlp_in.astype(b_type)
    w_qkv, w_dense, w_up, w_down = (
        lax.all_gather(qkv_weight.astype(b_type), "dp", axis=0, tiled=True),
        lax.all_gather(dense_weight.astype(b_type), "dp", axis=2, tiled=True),
        lax.all_gather(up_weight.astype(b_type), "dp", axis=0, tiled=True),
        lax.all_gather(down_weight.astype(b_type), "dp", axis=1, tiled=True),
    )
    qkv_flat = w_qkv.reshape(model_width, heads_here * 3 * head_size)
    dense_flat = w_dense.reshape(heads_here * head_size, model_width)
    key_full = jnp.concatenate([key_bias, jnp.zeros((heads_here, head_size - ROT), f_type)], axis=1)
    offset_full = jnp.stack([qv_bias[:, 0], key_full, qv_bias[:, 1]], axis=1)
    mixed_qkv = jnp.dot(attn_in, qkv_flat, preferred_element_type=f_type) + offset_full.reshape(-1)
    mixed_qkv = mixed_qkv.reshape(seq_count, length, heads_here, 3, head_size)
    cosine, sine_table = rope_tables(length)
    query_raw = mixed_qkv[..., 0, :]
    queries = rotate(query_raw, cosine, sine_table).astype(b_type)
    key_rows = rotate(mixed_qkv[..., 1, :], cosine, sine_table).astype(b_type)
    values = mixed_qkv[..., 2, :].astype(b_type)
    columns = jnp.arange(length, dtype=jnp.int32)

    def scores_at(seq_no, first_row):
        q_seq = lax.dynamic_index_in_dim(queries, seq_no, 0, keepdims=False)
        q_block = lax.dynamic_slice_in_dim(q_seq, first_row, QBLOCK, 0)
        key_seq = lax.dynamic_index_in_dim(key_rows, seq_no, 0, keepdims=False)
        value_seq = lax.dynamic_index_in_dim(values, seq_no, 0, keepdims=False)
        seg_row = lax.dynamic_index_in_dim(segment_ids, seq_no, 0, keepdims=False)
        seg_block = lax.dynamic_slice_in_dim(seg_row, first_row, QBLOCK, 0)
        row_ids = first_row + jnp.arange(QBLOCK, dtype=jnp.int32)
        scores = (
            jnp.einsum("qhd,khd->hqk", q_block, key_seq, preferred_element_type=f_type)
            * score_scale
        )
        allowed = (columns[None, :] <= row_ids[:, None]) & (seg_block[:, None] == seg_row[None, :])
        scores = jnp.where(allowed[None], scores, -1e30)
        return (q_block, key_seq, value_seq, scores)

    def forward_block(block_id):
        q_block, key_seq, value_seq, scores = scores_at(
            block_id // blocks, block_id % blocks * QBLOCK
        )
        row_max = jnp.max(scores, axis=-1, keepdims=True)
        expo = jnp.exp(scores - row_max)
        denominator = jnp.sum(expo, axis=-1, keepdims=True)
        probabilities = (expo / denominator).astype(b_type)
        context_block = jnp.einsum(
            "hqk,khd->qhd", probabilities, value_seq, preferred_element_type=f_type
        )
        return (context_block.astype(b_type), row_max[..., 0] + jnp.log(denominator[..., 0]))

    context, logsum = lax.map(forward_block, jnp.arange(block_count, dtype=jnp.int32))
    context_flat = context.reshape(row_count, heads_here * head_size)
    logsum = logsum.reshape(seq_count, blocks, heads_here, QBLOCK)
    attn_part = jnp.dot(context_flat, dense_flat, preferred_element_type=f_type)
    up_pre = jnp.dot(mlp_in, w_up, preferred_element_type=f_type) + up_bias
    activation = jax.nn.gelu(up_pre, approximate=False).astype(b_type)
    mlp_part = jnp.dot(activation, w_down, preferred_element_type=f_type)
    branch_sum = lax.psum(attn_part + mlp_part, "tensor")
    block_out = (inputs + branch_sum + dense_bias + down_bias).astype(b_type).reshape(tokens.shape)
    upstream = out_grad.reshape(row_count, model_width)
    bias_grad = jnp.sum(upstream.astype(f_type), axis=0)
    grad_down = jnp.einsum("nf,nd->fd", activation, upstream, preferred_element_type=f_type)
    act_grad = jnp.einsum("nd,fd->nf", upstream, w_down, preferred_element_type=f_type)
    pre_grad = (act_grad * gelu_slope(up_pre)).astype(b_type)
    grad_up = jnp.einsum("nd,nf->df", mlp_in, pre_grad, preferred_element_type=f_type)
    up_bias_grad = jnp.sum(pre_grad.astype(f_type), axis=0)
    mlp_in_grad = jnp.einsum("nf,df->nd", pre_grad, w_up, preferred_element_type=f_type)
    grad_dense = jnp.einsum("nc,nd->cd", context_flat, upstream, preferred_element_type=f_type)
    grad_dense = grad_dense.reshape(heads_here, head_size, model_width)
    context_grad = jnp.einsum(
        "nd,cd->nc", upstream, dense_flat, preferred_element_type=f_type
    ).astype(b_type)
    context_grad = context_grad.reshape(seq_count, length, heads_here, head_size)

    def sequence_back(seq_no):
        grad_seq = lax.dynamic_index_in_dim(context_grad, seq_no, 0, keepdims=False)
        logsum_seq = lax.dynamic_index_in_dim(logsum, seq_no, 0, keepdims=False)

        def block_step(state_pair, block_no):
            key_acc, value_acc = state_pair
            first_row = block_no * QBLOCK
            q_block, key_seq, value_seq, scores = scores_at(seq_no, first_row)
            grad_block = lax.dynamic_slice_in_dim(grad_seq, first_row, QBLOCK, 0)
            logsum_block = lax.dynamic_index_in_dim(logsum_seq, block_no, 0, keepdims=False)
            probabilities = jnp.exp(scores - logsum_block[:, :, None])
            value_acc = value_acc + jnp.einsum(
                "hqk,qhd->khd",
                probabilities.astype(b_type),
                grad_block,
                preferred_element_type=f_type,
            )
            prob_grad = jnp.einsum(
                "qhd,khd->hqk", grad_block, value_seq, preferred_element_type=f_type
            )
            centred = jnp.sum(probabilities * prob_grad, axis=-1, keepdims=True)
            score_grad = (probabilities * (prob_grad - centred)).astype(b_type)
            query_block = (
                jnp.einsum("hqk,khd->qhd", score_grad, key_seq, preferred_element_type=f_type)
                * score_scale
            )
            key_acc = (
                key_acc
                + jnp.einsum("hqk,qhd->khd", score_grad, q_block, preferred_element_type=f_type)
                * score_scale
            )
            return ((key_acc, value_acc), query_block)

        zero_grid = jnp.zeros((length, heads_here, head_size), f_type)
        (key_acc, value_acc), query_blocks = lax.scan(
            block_step, (zero_grid, zero_grid), jnp.arange(blocks, dtype=jnp.int32)
        )
        return (query_blocks.reshape(length, heads_here, head_size), key_acc, value_acc)

    query_grad, key_grad, value_grad = lax.map(
        sequence_back, jnp.arange(seq_count, dtype=jnp.int32)
    )
    rotated, unrotate = jax.vjp(lambda tensor: rotate(tensor, cosine, sine_table), query_raw)
    query_raw_grad = unrotate(query_grad)[0]
    key_raw_grad = unrotate(key_grad)[0]
    mixed_grad = jnp.stack([query_raw_grad, key_raw_grad, value_grad], axis=3).astype(b_type)
    mixed_flat = mixed_grad.reshape(row_count, heads_here * 3 * head_size)
    grad_qkv = jnp.einsum("nd,nc->dc", attn_in, mixed_flat, preferred_element_type=f_type)
    grad_qkv = grad_qkv.reshape(model_width, heads_here, 3, head_size)
    bias_sums = jnp.sum(mixed_grad.astype(f_type), axis=(0, 1))
    qv_grad = jnp.stack([bias_sums[:, 0], bias_sums[:, 2]], axis=1)
    key_bias_grad = bias_sums[:, 1, :ROT]
    attn_in_grad = jnp.einsum("nc,dc->nd", mixed_flat, qkv_flat, preferred_element_type=f_type)
    attn_full, mlp_full = lax.psum((attn_in_grad, mlp_in_grad), "tensor")
    attn_back, attn_gain_grad, attn_offset_grad = norm_back(
        attn_full, attn_hat, attn_inv, attn_norm_gain
    )
    mlp_back, mlp_gain_grad, mlp_offset_grad = norm_back(mlp_full, mlp_hat, mlp_inv, mlp_norm_gain)
    input_part = attn_back + mlp_back
    input_grad = (upstream.astype(f_type) + input_part).astype(b_type).reshape(tokens.shape)
    qkv_shard, dense_shard, up_shard, down_shard = (
        lax.psum_scatter(grad_qkv, "dp", scatter_dimension=0, tiled=True),
        lax.psum_scatter(grad_dense, "dp", scatter_dimension=2, tiled=True),
        lax.psum_scatter(grad_up, "dp", scatter_dimension=0, tiled=True),
        lax.psum_scatter(grad_down, "dp", scatter_dimension=1, tiled=True),
    )
    small_sums = lax.psum(
        (
            attn_gain_grad,
            attn_offset_grad,
            mlp_gain_grad,
            mlp_offset_grad,
            qv_grad,
            key_bias_grad,
            bias_grad,
            up_bias_grad,
        ),
        "dp",
    )
    return (
        block_out,
        input_grad,
        small_sums[0],
        small_sums[1],
        small_sums[2],
        small_sums[3],
        qkv_shard,
        small_sums[4],
        small_sums[5],
        dense_shard,
        small_sums[6],
        up_shard,
        small_sums[7],
        down_shard,
        small_sums[6],
    )


def solution(mesh):
    placed = (
        P("dp", None, None),
        P("dp", None),
        P("dp", None, None),
        P(),
        P(),
        P(),
        P(),
        P("dp", "tensor", None, None),
        P("tensor", None, None),
        P("tensor", None),
        P("tensor", None, "dp"),
        P(),
        P("dp", "tensor"),
        P("tensor"),
        P("tensor", "dp"),
        P(),
    )
    return jax.shard_map(
        body,
        mesh=mesh,
        in_specs=placed,
        out_specs=(
            P("dp", None, None),
            P("dp", None, None),
            P(),
            P(),
            P(),
            P(),
            P("dp", "tensor", None, None),
            P("tensor", None, None),
            P("tensor", None),
            P("tensor", None, "dp"),
            P(),
            P("dp", "tensor"),
            P("tensor"),
            P("tensor", "dp"),
            P(),
        ),
        check_vma=False,
    )
```

profile of v0, /device:TPU:0, one launch (start us, length us, event | category | flops | bytes accessed | tf_op | source)
XLA Modules:
  0.0 1771.7 jit_solution(15759231441247973863)
XLA Ops:
  9.2 3.3 copy.70
  16.7 3.0 convert_reduce_fusion
  22.7 41.7 %all-gather.7.cloned.1.call-done = bf16[2,256,2048]{2,1,0:T(8,128)(2,1)} async-done(((bf16[2,256,256]{2,1,0:T(8,128)(2,1)}), bf16[2,256,2048]{2,1,0:T(8,128)(2,1)}) %all-gather.7.cloned.1.call-update) | async-done | bytes 2097168 | tf_op jit(solution)/shard_map/all_gather | solution.py:83
  64.5 6.2 fusion.106
  70.7 94.5 %all-gather.5.cloned.1.call-done = bf16[2048,2,3,256]{0,3,2,1:T(8,128)(2,1)} async-done(((bf16[256,2,3,256]{0,3,2,1:T(8,128)(2,1)}), bf16[2048,2,3,256]{0,3,2,1:T(8,128)(2,1)}) %all-gather.5.cloned.1.call-update) | async-done | bytes 6291472 | tf_op jit(solution)/shard_map/all_gather | solution.py:82
  165.2 13.2 convolution_add_fusion
  178.5 6.6 copy.74
  207.0 19.5 %while.42 = (s32[]{:T(128)}, bf16[2,512,2,256]{3,2,1,0:T(2,128)(2,1)}, f32[2,2,512]{2,1,0:T(2,128)S(1)}, s32[2]{0:T(128)S(1)}, s32[1,1024]{1,0:T(1,128)S(1)}, /*...) while((s32[]{:T(128)}, ...), condition=%wide.region_5.6_spmd.clone, body=%wide.region_2.5_spmd.clone.sunk | while | flops 1088159232 | bytes 27310456 | solution.py:129
  226.5 29.4 %while.43 = (s32[]{:T(128)}, f32[1024,2,256]{0,2,1:T(8,128)S(1)}, f32[1024,2,256]{0,2,1:T(8,128)}, f32[2,512,2,256]{3,1,0,2:T(8,128)}, s32[2]{0:T(128)S(1)}, /*i...) while((s32[]{:T(128)}, f32[1024,2,256]{0,2,1:T(8,128)S(1)}, ...), condition=%wide.region_9.10_spmd.clone, body=%wide.region_7.9_spmd.clone.sunk | while | flops 2704539136 | bytes 94415344 | solution.py:187
  258.3 3.5 split.32
  273.9 9.1 fusion.128
  283.0 7.5 all-gather.9.cloned.1.call-done
  290.5 34.1 %fusion.79 = (bf16[1024,2048]{1,0:T(8,128)(2,1)}, f32[1024,2048]{1,0:T(8,128)}) fusion(f32[2048]{0:T(1024)S(1)} %copy-done.34, bf16[2048,2048]{1,0:T(8,128)(2,1)} %all-gather.9.cloned.1.call-done, bf16[1,1024,2048]{2,1,0:T(8,128)(2,1)} %param.20, f32[2048]{0:T(1024)S(1)} %copy-done.37, f32[2048]{0:T(1024)S(1)} %copy-done.25, f32[1024]{0:T(1024)S(1)} %add_rsqrt_fusion, ...), kind=kOutput, calls=%fused_computation.99 | convolution fusion | flops 8740929536 | bytes 25198592 | tf_op jit(solution)/shard_map/dot_general | solution.py:133
  324.6 91.3 %all-gather.11.cloned.1.call-done = bf16[2048,2048]{1,0:T(8,128)(2,1)} async-done(((bf16[2048,256]{1,0:T(8,128)(2,1)}), bf16[2048,2048]{1,0:T(8,128)(2,1)}) %all-gather.11.cloned.1.call-update) | async-done | bytes 8388624 | tf_op jit(solution)/shard_map/all_gather | solution.py:85
  416.0 12.6 fusion.127
  428.6 5.5 convolution_add_fusion.1
  434.1 16.6 convert_reduce_fusion.2
  450.8 12.9 fusion.129
  464.4 14.2 fusion.94
  479.2 6.6 fusion.96
  485.9 15.7 fusion.119
  501.6 15.6 fusion.98
  517.9 368.4 %all-reduce.13.cloned.1.call-done = (f32[1024,2048]{1,0:T(8,128)}, f32[1024,2048]{1,0:T(8,128)}, f32[1024,2048]{1,0:T(8,128)}) async-done(((f32[1024,2048]{1,0:T(8,128)}, f32[1024,2048]{1,0:T(8,128)}, f32[1024,2048]{1,0:T(8,128)}), (f32[1024,2048]{1,0:T(8,128)}, f32[1024,2048]{1,0:T(8,128)}, f32[1024,2048]{1,0:T(8,128)})) %all-reduce.13.cloned.1.call-update) | async-done | bytes 25165840 | tf_op jit(solution)/shard_map/psum | solution.py:136
  886.4 10.6 fusion.66
  897.0 3.5 copy-done.5
  900.5 12.5 convert_reduce_fusion.1
  913.0 41.6 %all-reduce.9 = (f32[2048]{0:T(1024)}, f32[2048]{0:T(1024)}, f32[2048]{0:T(1024)}, f32[2048]{0:T(1024)}, f32[2,2,256]{2,0,1:T(2,128)S(1)}, /*index=5*/f32[2,64]{1,0:T(2,128)}, f32[2048]{0:T(1024)S(1)}, f32[2048]{0:T(1024)}) all-reduce(f32[2048]{0:T(1024)S(1)} %get-tuple-element.420, ...), channel_id=1, replica_groups=mesh['dp'=8,'tensor'=4] {'dp'}, use_global_device_ids=true, to_apply=%region_17.18 | all-reduce | flops 13440 | bytes 107520 | tf_op jit(solution)/shard_map/psum | solution.py:219
  955.2 143.5 %reduce-scatter.5.cloned.1.call-done = f32[256,2,3,256]{3,0,2,1:T(8,128)} async-done(((f32[2048,2,3,256]{3,0,2,1:T(8,128)}), f32[256,2,3,256]{3,0,2,1:T(8,128)}) %reduce-scatter.5.cloned.1.call-update) | async-done | bytes 1572880 | tf_op jit(solution)/shard_map/reduce_scatter | solution.py:214
  1098.7 3.8 copy.90
  1102.5 88.4 %reduce-scatter.7.cloned.1.call-done = f32[2,256,256]{2,1,0:T(8,128)} async-done(((f32[2,256,2048]{2,1,0:T(8,128)}), f32[2,256,256]{2,1,0:T(8,128)}) %reduce-scatter.7.cloned.1.call-update) | async-done | bytes 524304 | tf_op jit(solution)/shard_map/reduce_scatter | solution.py:215
  1190.9 286.7 %reduce-scatter.9.cloned.1.call-done = f32[256,2048]{1,0:T(8,128)} async-done(((f32[2048,2048]{1,0:T(8,128)}), f32[256,2048]{1,0:T(8,128)}) %reduce-scatter.9.cloned.1.call-update) | async-done | bytes 2097168 | tf_op jit(solution)/shard_map/reduce_scatter | solution.py:216
  1477.7 286.7 %reduce-scatter.11.cloned.1.call-done = f32[2048,256]{1,0:T(8,128)} async-done(((f32[2048,2048]{1,0:T(8,128)}), f32[2048,256]{1,0:T(8,128)}) %reduce-scatter.11.cloned.1.call-update) | async-done | bytes 2097168 | tf_op jit(solution)/shard_map/reduce_scatter | solution.py:217
  (218 shorter events, 87.8 us)
Async XLA Ops:
  7.2 8.2 copy-start.17
  7.2 9.4 copy-start.33
  7.2 57.3 %all-gather.7.cloned.1.call-start = ((), (), s32[]{:S(2)}) async-start(), calls=%async_computation.5 | async-start | bytes 2359296 | tf_op jit(solution)/shard_map/all_gather | solution.py:83
  9.2 156.1 %all-gather.5.cloned.1.call-start = ((), (), s32[]{:S(2)}) async-start(), calls=%async_computation.4 | async-start | bytes 7077888 | tf_op jit(solution)/shard_map/all_gather | solution.py:82
  12.5 278.0 %all-gather.9.cloned.1.call-start = ((), (), s32[]{:S(2)}) async-start(), calls=%async_computation.6 | async-start | bytes 9437184 | tf_op jit(solution)/shard_map/all_gather | solution.py:84
  15.3 6.0 copy-start.32
  15.3 400.6 %all-gather.11.cloned.1.call-start = ((), (), s32[]{:S(2)}) async-start(), calls=%async_computation.7 | async-start | bytes 9437184 | tf_op jit(solution)/shard_map/all_gather | solution.py:85
  16.5 869.8 %all-reduce.13.cloned.1.call-start = ((), (), s32[]{:S(2)}) async-start(), calls=%async_computation.12 | async-start | bytes 50331648 | tf_op jit(solution)/shard_map/psum | solution.py:136
  16.6 3.5 copy-start
  64.5 100.8 %copy-start.26 = (f32[2048]{0:T(1024)S(1)}, f32[2048]{0:T(1024)}, u32[]{:S(2)}) copy-start(f32[2048]{0:T(1024)} %param.23) | copy-start | bytes 24580
  64.5 100.8 %copy-start.35 = (f32[2048]{0:T(1024)S(1)}, f32[2048]{0:T(1024)}, u32[]{:S(2)}) copy-start(f32[2048]{0:T(1024)} %param.24) | copy-start | bytes 24580
  195.5 11.5 copy-start.24
  249.3 3.5 copy-start.19
  256.0 5.9 copy-start.23
  269.5 4.4 slice-start.2
  273.9 16.6 copy-start.25
  273.9 16.6 copy-start.34
  273.9 16.6 copy-start.37
  416.0 12.6 copy-start.16
  428.6 5.6 copy-start.14
  428.6 22.2 %slice-start = ((s8[8388608]{0:T(1024)(128)(4,1)}), s8[4194304]{0:T(1024)(128)(4,1)S(1)}, s32[]{:S(2)}) async-start(s8[8388608]{0:T(1024)(128)(4,1)} %bitcast.266), calls=%async_computation.13 | async-start | bytes 8388608
  434.1 16.6 slice-start.1
  463.7 635.1 %reduce-scatter.5.cloned.1.call-start = ((), (), s32[]{:S(2)}) async-start(), calls=%async_computation.8 | async-start | bytes 14155776 | tf_op jit(solution)/shard_map/reduce_scatter | solution.py:214
  478.6 712.3 %reduce-scatter.7.cloned.1.call-start = ((), (), s32[]{:S(2)}) async-start(), calls=%async_computation.9 | async-start | bytes 4718592 | tf_op jit(solution)/shard_map/reduce_scatter | solution.py:215
  485.8 991.9 %reduce-scatter.9.cloned.1.call-start = ((), (), s32[]{:S(2)}) async-start(), calls=%async_computation.10 | async-start | bytes 18874368 | tf_op jit(solution)/shard_map/reduce_scatter | solution.py:216
  501.6 1262.8 %reduce-scatter.11.cloned.1.call-start = ((), (), s32[]{:S(2)}) async-start(), calls=%async_computation.11 | async-start | bytes 18874368 | tf_op jit(solution)/shard_map/reduce_scatter | solution.py:217
  886.3 10.7 copy-start.1
  886.3 10.7 copy-start.4
  886.3 14.2 copy-start.5
  886.3 14.2 copy-start.29
  886.3 14.2 copy-start.30
  954.6 810.4 %copy-start.31 = (f32[2048]{0:T(1024)}, f32[2048]{0:T(1024)S(1)}, u32[]{:S(2)}) copy-start(f32[2048]{0:T(1024)S(1)} %get-tuple-element.758) | copy-start | bytes 24580
  (28 other events, 54.3 us)
Sparse Core Ops, SparseCore 0:
  10.7 53.7 all-gather.6
  67.1 98.1 all-gather.4
  167.4 123.1 all-gather.8
  292.4 123.4 all-gather.10
  463.8 422.4 all-reduce.12
  890.2 208.4 reduce-scatter.4
  1103.4 87.5 reduce-scatter.6
  1195.3 282.3 reduce-scatter.8
  1482.5 281.7 reduce-scatter.10
where the time goes:
time: 1780 us; the launch traced here: 1770 us
  waiting for transfers between devices  1410 us (79%)
  matrix products  186 us (10%)
  local copies, waits for them, and re-layouts  57.5 us (3%)
  other arithmetic  52.3 us (3%)
  blocking collectives  41.6 us (2%)
    psum x1, waiting for transfers between devices, body(): branch_sum = lax.psum(attn_part + mlp_part, 'tensor')  368 us
    reduce_scatter x1, waiting for transfers between devices, body(): lax.psum_scatter(grad_up, 'dp', scatter_dimension=0, tiled=True)  287 us
    reduce_scatter x1, waiting for transfers between devices, body(): lax.psum_scatter(grad_down, 'dp', scatter_dimension=1, tiled=True)  287 us
    reduce_scatter x1, waiting for transfers between devices, body(): lax.psum_scatter(grad_qkv, 'dp', scatter_dimension=0, tiled=True)  144 us
    all_gather x1, waiting for transfers between devices, body(): lax.all_gather(qkv_weight.astype(b_type), 'dp', axis=0, tiled=True)  94.5 us
    all_gather x1, waiting for transfers between devices, body(): lax.all_gather(down_weight.astype(b_type), 'dp', axis=1, tiled=True)  91.3 us
    reduce_scatter x1, waiting for transfers between devices, body(): lax.psum_scatter(grad_dense, 'dp', scatter_dimension=2, tiled=True)  88.4 us
    all_gather x1, waiting for transfers between devices, body(): lax.all_gather(dense_weight.astype(b_type), 'dp', axis=2, tiled=True)  41.7 us
  transfers between devices with their start and end apart: 9, of which 9 were waited for; matrix products, arithmetic and copies ran while one was open for 13% of the time, Pallas kernels for 0%

commit v1 on v0

v1 whole, which is shorter than its diff:
```python
import jax
import jax.numpy as jnp
from jax import lax
from jax.experimental import pallas as pl
from jax.experimental.pallas import tpu as pltpu
from jax.sharding import PartitionSpec as P

ROT = 64
PAIR = 2
QBLOCK = 256
DOC_MAX = 512
F = jnp.float32
B = jnp.bfloat16


def dot(left, right, dims, kind):
    return lax.dot_general(left, right, (dims, ((), ())), preferred_element_type=F).astype(kind)


def gelu_slope(pre_act):
    cumulative = 0.5 * (1.0 + lax.erf(pre_act * 0.7071067811865476))
    density = jnp.exp(-0.5 * pre_act * pre_act) * 0.3989422804014327
    return cumulative + pre_act * density


def rope_tables(length):
    half = ROT // 2
    frequency = 10000.0 ** (-(jnp.arange(half, dtype=F) * 2.0) / ROT)
    angles = jnp.arange(length, dtype=F)[:, None] * frequency[None, :]
    cosine, sine = jnp.cos(angles), jnp.sin(angles)
    flat = jnp.zeros((length, 128 - ROT), F)
    zero = jnp.zeros_like(sine)
    return (
        jnp.concatenate([cosine, cosine, flat + 1.0], axis=1),
        jnp.concatenate([-sine, zero, flat], axis=1),
        jnp.concatenate([zero, sine, flat], axis=1),
    )


def turn(rows, cosine, from_above, from_below):
    head = rows[:, :128]
    above = pltpu.roll(head, 128 - ROT // 2, 1)
    below = pltpu.roll(head, ROT // 2, 1)
    turned = head * cosine + above * from_above + below * from_below
    return jnp.concatenate([turned, rows[:, 128:]], axis=1)


def block_mask(seg_col_ref, seg_row_ref, first, low, high):
    rows = first + lax.broadcasted_iota(jnp.int32, (QBLOCK, high - low), 0)
    columns = low + lax.broadcasted_iota(jnp.int32, (QBLOCK, high - low), 1)
    same = seg_col_ref[0, first : first + QBLOCK, :] == seg_row_ref[0, :, low:high]
    return (columns <= rows) & same


def key_range(first):
    return max(0, first - DOC_MAX), first + QBLOCK


def attn_forward(mixed_ref, bias_ref, cos_ref, up_ref, down_ref, col_ref, row_ref, q_ref, k_ref, v_ref, ctx_ref, lse_ref):
    size = q_ref.shape[2]
    length = q_ref.shape[1]
    scale = size ** (-0.5)
    tables = (cos_ref[...], up_ref[...], down_ref[...])
    q_ref[0] = turn(mixed_ref[0, :, :size] + bias_ref[:, :size], *tables).astype(B)
    k_ref[0] = turn(mixed_ref[0, :, size : 2 * size] + bias_ref[:, size : 2 * size], *tables).astype(B)
    v_ref[0] = (mixed_ref[0, :, 2 * size :] + bias_ref[:, 2 * size :]).astype(B)
    for first in range(0, length, QBLOCK):
        low, high = key_range(first)
        scores = dot(q_ref[0, first : first + QBLOCK], k_ref[0, low:high], ((1,), (1,)), F) * scale
        scores = jnp.where(block_mask(col_ref, row_ref, first, low, high), scores, -1e30)
        row_max = jnp.max(scores, axis=1, keepdims=True)
        expo = jnp.exp(scores - row_max)
        total = jnp.sum(expo, axis=1, keepdims=True)
        probs = (expo / total).astype(B)
        ctx_ref[0, first : first + QBLOCK] = dot(probs, v_ref[0, low:high], ((1,), (0,)), B)
        lse_ref[0, first : first + QBLOCK] = row_max + jnp.log(total)


def attn_backward(q_ref, k_ref, v_ref, grad_ref, lse_ref, cos_ref, up_ref, down_ref, col_ref, row_ref, mixed_ref, sum_ref, q_acc, k_acc, v_acc):
    size = q_ref.shape[2]
    length = q_ref.shape[1]
    scale = size ** (-0.5)
    k_acc[...] = jnp.zeros_like(k_acc)
    v_acc[...] = jnp.zeros_like(v_acc)
    for first in range(0, length, QBLOCK):
        low, high = key_range(first)
        here = slice(first, first + QBLOCK)
        scores = dot(q_ref[0, here], k_ref[0, low:high], ((1,), (1,)), F) * scale
        scores = jnp.where(block_mask(col_ref, row_ref, first, low, high), scores, -1e30)
        probs = jnp.exp(scores - lse_ref[0, here])
        v_acc[low:high] += dot(probs.astype(B), grad_ref[0, here], ((0,), (0,)), F)
        prob_grad = dot(grad_ref[0, here], v_ref[0, low:high], ((1,), (1,)), F)
        centred = jnp.sum(probs * prob_grad, axis=1, keepdims=True)
        score_grad = (probs * (prob_grad - centred)).astype(B)
        q_acc[here] = dot(score_grad, k_ref[0, low:high], ((1,), (0,)), F) * scale
        k_acc[low:high] += dot(score_grad, q_ref[0, here], ((0,), (0,)), F) * scale
    tables = (cos_ref[...], -up_ref[...], -down_ref[...])
    q_grad = turn(q_acc[...], *tables).astype(B)
    k_grad = turn(k_acc[...], *tables).astype(B)
    v_grad = v_acc[...].astype(B)
    for number, part in enumerate((q_grad, k_grad, v_grad)):
        mixed_ref[0, :, number * size : (number + 1) * size] = part
        sum_ref[0, :, number * size : (number + 1) * size] = jnp.sum(part.astype(F), axis=0, keepdims=True)


def per_seq(rows, columns):
    return pl.BlockSpec((1, rows, columns), lambda seq: (seq, 0, 0))


def shared(rows, columns):
    return pl.BlockSpec((rows, columns), lambda seq: (0, 0))


def body(
    tokens,
    segment_ids,
    out_grad,
    attn_norm_gain,
    attn_norm_bias,
    mlp_norm_gain,
    mlp_norm_bias,
    qkv_weight,
    qv_bias,
    key_bias,
    dense_weight,
    dense_bias,
    up_weight,
    up_bias,
    down_weight,
    down_bias,
    *,
    groups,
    ways,
):
    length, width = tokens.shape[1:]
    heads, size = qkv_weight.shape[1] // 2, qkv_weight.shape[3]
    part = width // groups
    me = lax.axis_index("dp")
    half = (me // PAIR) % 2
    place = lax.axis_index("tensor")
    core, side = place % 2, place // 2
    spread = [bit for bit in (1 << k for k in reversed(range(groups.bit_length() - 1))) if bit != PAIR]

    def swap(array, bit):
        return lax.ppermute(array, "dp", [(i, i ^ bit) for i in range(groups)])

    def cross(array, bit):
        return lax.ppermute(array, "tensor", [(i, i ^ bit) for i in range(ways)])

    def pick(array, index, axis, count=2):
        rows = array.shape[axis] // count
        return lax.dynamic_slice_in_dim(array, index * rows, rows, axis)

    def join(mine, theirs, index, axis):
        pair = jnp.concatenate([mine, theirs], axis=axis)
        turned = jnp.concatenate([theirs, mine], axis=axis)
        return jnp.where(index == 0, pair, turned)

    order = [0, PAIR]
    for bit in spread:
        order = order + [mask | bit for mask in order]
    inverse = [order.index(mask) for mask in range(groups)]

    def arranged(array):
        return jnp.concatenate(
            [lax.dynamic_slice_in_dim(array, (mask ^ me) * part, part, array.ndim - 1) for mask in order], axis=-1
        )

    def natural(array):
        table = jnp.asarray(inverse, jnp.int32)
        return jnp.concatenate(
            [lax.dynamic_slice_in_dim(array, table[block ^ me] * part, part, array.ndim - 1) for block in range(groups)],
            axis=-1,
        )

    def gather(shard, halves_axis, axis):
        shard = shard.astype(B)
        mine, theirs = pick(shard, half, halves_axis), pick(shard, 1 - half, halves_axis)
        pieces = [jnp.concatenate([mine, swap(theirs, PAIR)], axis=axis)]
        for bit in spread:
            pieces = pieces + [swap(piece, bit) for piece in pieces]
        return jnp.concatenate(pieces, axis=axis)

    def scatter(product, axis, halves_axis):
        count = groups // 2
        sent = swap(product(count, groups, B), spread[-1])
        held = product(0, count, F) + sent.astype(F)
        for bit in reversed(spread[:-1]):
            keep, send = jnp.split(held, 2, axis=axis)
            held = keep + swap(send.astype(B), bit).astype(F)
        keep, send = jnp.split(held, 2, axis=axis)
        return join(keep, swap(send, PAIR), half, halves_axis)

    def share_rows(rows):
        rows = join(rows, cross(rows, 2), side, 0)
        return join(rows, cross(rows, 1), core, 0)

    def own_rows(array, axis):
        return pick(pick(array, core, axis), side, axis)

    def partner_rows(array):
        return share_rows(swap(own_rows(array, 0), PAIR))

    def total_rows(partial):
        held = pick(partial, core, 1).astype(F) + cross(pick(partial, 1 - core, 1), 1).astype(F)
        held = pick(held, side, 1) + cross(pick(held, 1 - side, 1).astype(B), 2).astype(F)
        sent = swap(held[1].astype(B), PAIR).astype(F)
        rows = sent.shape[0]
        sent = jnp.flip(sent.reshape(rows, groups // 2, 2, part), axis=2).reshape(rows, width)
        return held[0] + sent

    own_x, own_g = tokens[0], out_grad[0]
    w_up = gather(up_weight, 1, 0)
    x_other = partner_rows(own_x)
    w_down = gather(down_weight, 0, 1)
    g_other = partner_rows(own_g)
    w_qkv = gather(qkv_weight.reshape(part, 2, -1), 1, 0).reshape(width, -1)
    w_dense = gather(dense_weight.reshape(2 * heads * size, part), 0, 1)

    x_pair = arranged(jnp.concatenate([own_x, x_other], axis=0))
    g_pair = arranged(jnp.concatenate([own_g, g_other], axis=0))
    gains = [arranged(v) for v in (attn_norm_gain, attn_norm_bias, mlp_norm_gain, mlp_norm_bias)]

    def hat(rows):
        rows = rows.astype(F)
        center = rows - jnp.mean(rows, axis=-1, keepdims=True)
        inverse_dev = lax.rsqrt(jnp.mean(center * center, axis=-1, keepdims=True) + 1e-05)
        return center * inverse_dev, inverse_dev

    normed, _ = hat(x_pair)
    attn_in = (normed * gains[0] + gains[1]).astype(B)
    mlp_in = (normed * gains[2] + gains[3]).astype(B)

    up_here = pick(up_bias, half, 0)
    up_pre = dot(mlp_in, w_up, ((1,), (0,)), F) + up_here
    activation = jax.nn.gelu(up_pre, approximate=False).astype(B)
    middle = width // 2

    def columns(array, low, high):
        return array[:, low * part : high * part]

    down_shard = scatter(lambda low, high, kind: dot(activation, columns(g_pair, low, high), ((0,), (0,)), kind), 1, 0)
    pre_grad = (dot(g_pair, w_down, ((1,), (1,)), F) * gelu_slope(up_pre)).astype(B)
    up_shard = scatter(lambda low, high, kind: dot(columns(mlp_in, low, high), pre_grad, ((0,), (0,)), kind), 0, 1)
    up_bias_sum = jnp.sum(pre_grad.astype(F), axis=0)

    seg_other = swap(segment_ids[0], PAIR)
    seg = jnp.stack([segment_ids[0], seg_other])
    seg_col, seg_row = seg[:, :, None], seg[:, None, :]
    qv_here, key_here = pick(qv_bias, half, 0), pick(key_bias, half, 0)
    key_full = jnp.concatenate([key_here, jnp.zeros((heads, size - ROT), F)], axis=1)
    offsets = jnp.stack([qv_here[:, 0], key_full, qv_here[:, 1]], axis=1).reshape(heads, 1, 3 * size)
    mixed = dot(attn_in, w_qkv, ((1,), (0,)), F).reshape(2, length, heads, 3 * size)
    tables = rope_tables(length)
    table_specs = [shared(length, 128)] * 3
    seg_specs = [per_seq(length, 1), per_seq(1, length)]
    context_grad = dot(g_pair, w_dense, ((1,), (1,)), B).reshape(2, length, heads, size)
    contexts, mixed_grads, mixed_sums = [], [], []
    head_shape = jax.ShapeDtypeStruct((2, length, size), B)
    for head in range(heads):
        q, k, v, context, lse = pl.pallas_call(
            attn_forward,
            grid=(2,),
            in_specs=[per_seq(length, 3 * size), shared(1, 3 * size)] + table_specs + seg_specs,
            out_specs=[per_seq(length, size)] * 4 + [per_seq(length, 1)],
            out_shape=[head_shape] * 4 + [jax.ShapeDtypeStruct((2, length, 1), F)],
            name="attn_forward",
        )(mixed[:, :, head], offsets[head], *tables, seg_col, seg_row)
        mixed_grad, mixed_sum = pl.pallas_call(
            attn_backward,
            grid=(2,),
            in_specs=[per_seq(length, size)] * 4 + [per_seq(length, 1)] + table_specs + seg_specs,
            out_specs=[per_seq(length, 3 * size), per_seq(1, 3 * size)],
            out_shape=[
                jax.ShapeDtypeStruct((2, length, 3 * size), B),
                jax.ShapeDtypeStruct((2, 1, 3 * size), F),
            ],
            scratch_shapes=[pltpu.VMEM((length, size), F)] * 3,
            name="attn_backward",
        )(q, k, v, context_grad[:, :, head], lse, *tables, seg_col, seg_row)
        contexts.append(context.reshape(2 * length, size))
        mixed_grads.append(mixed_grad.reshape(2 * length, 3 * size))
        mixed_sums.append(jnp.sum(mixed_sum, axis=(0, 1)))
    context = jnp.concatenate(contexts, axis=1)
    mixed_grad = jnp.concatenate(mixed_grads, axis=1)
    mixed_sum = jnp.stack(mixed_sums).reshape(heads, 3, size)

    qkv_shard = scatter(lambda low, high, kind: dot(columns(attn_in, low, high), mixed_grad, ((0,), (0,)), kind), 0, 1)
    dense_shard = scatter(lambda low, high, kind: dot(context, columns(g_pair, low, high), ((0,), (0,)), kind), 1, 0)

    branch = dot(context, w_dense, ((1,), (0,)), F) + dot(activation, w_down, ((1,), (0,)), F)
    branch_rows = total_rows(branch.astype(B).reshape(2, length, width))
    x_rows, g_rows = own_rows(x_pair[:length], 0), own_rows(g_pair[:length], 0)
    out_rows = (x_rows.astype(F) + branch_rows + arranged(dense_bias) + arranged(down_bias)).astype(B)
    block_out = share_rows(natural(out_rows))

    attn_in_grad = dot(mixed_grad, w_qkv, ((1,), (1,)), F)
    mlp_in_grad = dot(pre_grad, w_up, ((1,), (1,)), F)
    blend = (attn_in_grad * gains[0] + mlp_in_grad * gains[2]).astype(B)
    blend_rows = total_rows(blend.reshape(2, length, width))
    hat_rows, inverse_rows = hat(x_rows)
    inner = (
        blend_rows
        - jnp.mean(blend_rows, axis=-1, keepdims=True)
        - hat_rows * jnp.mean(blend_rows * hat_rows, axis=-1, keepdims=True)
    )
    input_grad = share_rows(natural((g_rows.astype(F) + inner * inverse_rows).astype(B)))

    norm_sums = natural(
        jnp.stack(
            [
                jnp.sum(attn_in_grad * normed, axis=0),
                jnp.sum(attn_in_grad, axis=0),
                jnp.sum(mlp_in_grad * normed, axis=0),
                jnp.sum(mlp_in_grad, axis=0),
            ]
        )
    ).reshape(-1)
    bias_sum = jnp.sum(own_g.astype(F), axis=0)

    def slotted(array):
        zero = jnp.zeros_like(array)
        return join(array, zero, half, 0)

    small = [norm_sums, bias_sum, slotted(up_bias_sum), slotted(mixed_sum).reshape(-1)]
    sizes = [s.shape[0] for s in small]
    flat = jnp.concatenate(small)
    for bit in [1 << k for k in range(groups.bit_length() - 1)]:
        flat = flat + swap(flat, bit)
    ends = [sum(sizes[: i + 1]) for i in range(len(sizes))]
    norms = flat[: ends[0]]
    for bit in [1 << k for k in range(ways.bit_length() - 1)]:
        norms = norms + cross(norms, bit)
    norms = norms.reshape(4, width)
    bias_grad = flat[ends[0] : ends[1]]
    up_bias_grad = flat[ends[1] : ends[2]]
    mixed_bias = flat[ends[2] :].reshape(2 * heads, 3, size)
    qv_grad = jnp.stack([mixed_bias[:, 0], mixed_bias[:, 2]], axis=1)
    key_bias_grad = mixed_bias[:, 1, :ROT]

    return (
        block_out[None],
        input_grad[None],
        norms[0],
        norms[1],
        norms[2],
        norms[3],
        qkv_shard.reshape(qkv_weight.shape),
        qv_grad,
        key_bias_grad,
        dense_shard.reshape(dense_weight.shape),
        bias_grad,
        up_shard,
        up_bias_grad,
        down_shard,
        bias_grad,
    )


def solution(mesh):
    placed = (
        P("dp", None, None),
        P("dp", None),
        P("dp", None, None),
        P(),
        P(),
        P(),
        P(),
        P("dp", "tensor", None, None),
        P("tensor", None, None),
        P("tensor", None),
        P("tensor", None, "dp"),
        P(),
        P("dp", "tensor"),
        P("tensor"),
        P("tensor", "dp"),
        P(),
    )

    def whole(*arrays):
        return body(*arrays, groups=mesh.shape["dp"], ways=mesh.shape["tensor"])

    return jax.shard_map(
        whole,
        mesh=mesh,
        in_specs=placed,
        out_specs=(
            P("dp", None, None),
            P("dp", None, None),
            P(),
            P(),
            P(),
            P(),
            P("dp", "tensor", None, None),
            P("tensor", None, None),
            P("tensor", None),
            P("tensor", None, "dp"),
            P(),
            P("dp", "tensor"),
            P("tensor"),
            P("tensor", "dp"),
            P(),
        ),
        check_vma=False,
    )
```

time: 1780 us -> 859 us (0.48)
  waiting for transfers between devices: 1410 us -> 330 us
  local copies, waits for them, and re-layouts: 57.5 us -> 163 us
  other arithmetic: 52.3 us -> 115 us
  starting transfers between devices: 0.37 us -> 42 us
  blocking collectives: 41.6 us -> 0 us
  Pallas kernels: 0 us -> 21.8 us
  matrix products: 186 us -> 168 us
    reduce_scatter x4 -> x0, waiting for transfers between devices: 805 us -> none  [the longest x1 287 us: body(): lax.psum_scatter(grad_up, 'dp', scatter_dimension=0, tiled=True)]
    psum x1 -> x0, waiting for transfers between devices: 368 us -> none  [body(): branch_sum = lax.psum(attn_part + mlp_part, 'tensor')]
    ppermute x0 -> x50, waiting for transfers between devices: none -> 330 us  [the longest x36 266 us: swap(): return lax.ppermute(array, 'dp', [(i, i ^ bit) for i in range(groups)])]
    all_gather x4 -> x0, waiting for transfers between devices: 235 us -> none  [the longest x1 94.5 us: body(): lax.all_gather(qkv_weight.astype(b_type), 'dp', axis=0, tiled=True)]
    unnamed x78 -> x278, local copies, waits for them, and re-layouts: 27.7 us -> 88.3 us
    ppermute x0 -> x50, starting transfers between devices: none -> 42 us  [the longest x36 33.2 us: swap(): return lax.ppermute(array, 'dp', [(i, i ^ bit) for i in range(groups)])]
    psum x1 -> x0, blocking collectives: 41.6 us -> none  [body(): lax.psum((attn_gain_grad, attn_offset_grad, mlp_gain_grad, mlp_offset_gra...]
    select_n x0 -> x14, other arithmetic: none -> 40.4 us  [join(): return jnp.where(index == 0, pair, turned)]
  transfers between devices with their start and end apart: 9 -> 50, of which waited for: 9 -> 21; matrix products, arithmetic and copies ran while one was open for 13% -> 34% of each run, Pallas kernels for 0% -> 1%
where the time goes in v1:
time: 859 us; the launch traced here: 847 us
  waiting for transfers between devices  330 us (38%)
  matrix products  168 us (20%)
  local copies, waits for them, and re-layouts  163 us (19%)
  other arithmetic  115 us (13%)
  starting transfers between devices  42 us (5%)
  Pallas kernels  21.8 us (3%)
    ppermute x36, waiting for transfers between devices, swap(): return lax.ppermute(array, 'dp', [(i, i ^ bit) for i in range(groups)])  266 us
    dot_general x16, matrix products, dot(): lax.dot_general(left, right, (dims, ((), ())), preferred_element_type=F)  168 us
    unnamed x278, local copies, waits for them, and re-layouts  88.3 us
    ppermute x14, waiting for transfers between devices, cross(): return lax.ppermute(array, 'tensor', [(i, i ^ bit) for i in range(ways)])  64.2 us
    select_n x14, other arithmetic, join(): return jnp.where(index == 0, pair, turned)  40.4 us
    ppermute x36, starting transfers between devices, swap(): return lax.ppermute(array, 'dp', [(i, i ^ bit) for i in range(groups)])  33.2 us
  transfers between devices with their start and end apart: 50, of which 21 were waited for; matrix products, arithmetic and copies ran while one was open for 34% of the time, Pallas kernels for 1%

profile of v1, /device:TPU:0, one launch (start us, length us, event | category | flops | bytes accessed | tf_op | source)
XLA Modules:
  0.0 847.5 jit_solution(5757791769696616406)
XLA Ops:
  90.1 10.0 %collective-permute-done.9 = bf16[256,512]{1,0:T(8,128)(2,1)S(1)} collective-permute-done((bf16[256,512]{1,0:T(8,128)(2,1)}, bf16[256,512]{1,0:T(8,128)(2,1)S(1)}, u32[]{:S(2)}, u32[]{:S(2)}) %collective-permute-start.9) | collective-permute-done | bytes 262176 | tf_op jit(solution)/shard_map/ppermute | solution.py:145
  129.7 51.1 %collective-permute-done.4 = bf16[512,1,768]{2,0,1:T(8,128)(2,1)} collective-permute-done((bf16[512,1,768]{2,0,1:T(8,128)(2,1)}, bf16[512,1,768]{2,0,1:T(8,128)(2,1)}, u32[]{:S(2)}, u32[]{:S(2)}) %collective-permute-start.4) | collective-permute-done | bytes 786464 | tf_op jit(solution)/shard_map/ppermute | solution.py:145
  188.2 26.3 %collective-permute-done.13 = bf16[512,1024]{1,0:T(8,128)(2,1)S(1)} collective-permute-done((bf16[512,1024]{1,0:T(8,128)(2,1)S(1)}, bf16[512,1024]{1,0:T(8,128)(2,1)S(1)}, u32[]{:S(2)}, u32[]{:S(2)}) %collective-permute-start.13) | collective-permute-done | bytes 1048608 | tf_op jit(solution)/shard_map/ppermute | solution.py:145
  220.4 14.6 %collective-permute-done.17 = bf16[1024,512]{1,0:T(8,128)(2,1)S(1)} collective-permute-done((bf16[1024,512]{1,0:T(8,128)(2,1)S(1)}, bf16[1024,512]{1,0:T(8,128)(2,1)S(1)}, u32[]{:S(2)}, u32[]{:S(2)}) %collective-permute-start.17) | collective-permute-done | bytes 1048608 | tf_op jit(solution)/shard_map/ppermute | solution.py:145
  241.3 19.8 %collective-permute-done.15 = bf16[512,1024]{1,0:T(8,128)(2,1)S(1)} collective-permute-done((bf16[512,1024]{1,0:T(8,128)(2,1)S(1)}, bf16[512,1024]{1,0:T(8,128)(2,1)S(1)}, u32[]{:S(2)}, u32[]{:S(2)}) %collective-permute-start.15) | collective-permute-done | bytes 1048608 | tf_op jit(solution)/shard_map/ppermute | solution.py:145
  261.2 19.6 %collective-permute-done.19 = bf16[1024,512]{1,0:T(8,128)(2,1)S(1)} collective-permute-done((bf16[1024,512]{1,0:T(8,128)(2,1)S(1)}, bf16[1024,512]{1,0:T(8,128)(2,1)S(1)}, u32[]{:S(2)}, u32[]{:S(2)}) %collective-permute-start.19) | collective-permute-done | bytes 1048608 | tf_op jit(solution)/shard_map/ppermute | solution.py:145
  321.1 6.7 fusion.7
  327.8 27.8 %fusion.15 = (bf16[2048,1024]{1,0:T(8,128)(2,1)}, f32[2048,1024]{1,0:T(8,128)}) fusion(f32[1024]{0:T(1024)S(1)} %dynamic_slice.469, bf16[2048,2048]{1,0:T(8,128)(2,1)S(1)} %fusion.7, bf16[2048,1024]{1,0:T(8,128)(2,1)S(1)} %copy-done.55), kind=kOutput, calls=%fused_computation.54 | convolution fusion | flops 8728346624 | bytes 25169920 | tf_op jit(solution)/shard_map/dot_general | solution.py:17
  355.6 17.4 %convert_reduce_fusion.1 = (f32[1024]{0:T(1024)S(1)}, bf16[2048,1024]{1,0:T(8,128)(2,1)}) fusion(f32[2048,1024]{1,0:T(8,128)} %get-tuple-element.148, f32[1024]{0:T(1024)S(1)} %dynamic_slice.469, bf16[2048,2048]{1,0:T(8,128)(2,1)S(1)} %bitcast.139, bf16[1024,2048]{1,0:T(8,128)(2,1)} %copy-done.58), kind=kOutput, calls=%fused_computation.62 | convolution fusion | flops 8617196544 | bytes 25174016 | tf_op jit(solution)/shard_map/dot_general | solution.py:17
  373.1 8.1 fusion.60
  381.2 11.7 %fusion.121 = f32[2048,2048]{1,0:T(8,128)} fusion(bf16[2048,1024]{1,0:T(8,128)(2,1)S(1)} %copy-done.80, bf16[2048,1024]{1,0:T(8,128)(2,1)S(1)} %copy-done.56), kind=kOutput, calls=%fused_computation.355 | convolution fusion | flops 8589934592 | bytes 25165824 | tf_op jit(solution)/shard_map/dot_general | solution.py:17
  398.2 11.9 %fusion.120 = f32[2048,2048]{1,0:T(8,128)} fusion(bf16[2048,1024]{1,0:T(8,128)(2,1)S(1)} %copy-done.81, bf16[1024,2048]{1,0:T(8,128)(2,1)S(1)} %copy-done.59), kind=kOutput, calls=%fused_computation.354 | convolution fusion | flops 8589934592 | bytes 25165824 | tf_op jit(solution)/shard_map/dot_general | solution.py:17
  420.0 9.6 %fusion.22.mixed_ref = f32[2,1024,768]{2,1,0:T(8,128)} fusion(bf16[2,1024,2048]{2,1,0:T(8,128)(2,1)S(1)} %constant_dynamic-update-slice_fusion.8, f32[2048]{0:T(1024)S(1)} %copy-done.78, f32[2048]{0:T(1024)S(1)} %copy-done.79, f32[2,1024]{1,0:T(2,128)S(1)} %copy-done.72, f32[2,1024]{1,0:T(2,128)S(1)} %copy-done.71, bf16[2048,1,768]{2,0,1:T(8,128)(2,1)S(1)} %copy-done.62), kind=kOutput, calls=%fused_computation.61 | convolution fusion | flops 6467616768 | bytes 17858560 | tf_op jit(solution)/shard_map/dot_general | solution.py:17
  429.7 10.9 %attn_forward.1 = (bf16[2,1024,256]{2,1,0:T(8,128)(2,1)}, bf16[2,1024,256]{2,1,0:T(8,128)(2,1)}, bf16[2,1024,256]{2,1,0:T(8,128)(2,1)}, bf16[2,1024,256]{2,1,0:T(8,128)(2,1)}, f32[2,1024,1]{2,1,0:T(8,128)}) custom-call(f32[2,1024,768]{2,1,0:T(8,128)} %fusion.22.mixed_ref, f32[1,768]{1,0:T(1,128)} %bitcast.153, f32[1024,128]{1,0:T(8,128)} %maximum_maximum_fusion.cos_ref, ...), custom_call_target="tpu_custom_call" | custom-call | tf_op jit(solution)/shard_map/attn_forward/pallas_call | solution.py:261
  446.8 6.8 convolution_convert_fusion
  453.6 10.9 %attn_backward.1 = (bf16[2,1024,768]{2,1,0:T(8,128)(2,1)}, f32[2,1,768]{2,1,0:T(1,128)}) custom-call(bf16[2,1024,256]{2,1,0:T(8,128)(2,1)} %get-tuple-element.23.q_ref, bf16[2,1024,256]{2,1,0:T(8,128)(2,1)} %get-tuple-element.24.k_ref, bf16[2,1024,256]{2,1,0:T(8,128)(2,1)} %get-tuple-element.25.v_ref, bf16[2,1024,256]{2,1,0:T(8,128)(2,1)} %bitcast.144, ...), custom_call_target="tpu_custom_call" | custom-call | tf_op jit(solution)/shard_map/attn_backward/pallas_call | solution.py:269
  464.6 22.6 %fusion.8 = (f32[2048]{0:T(1024)S(1)}, f32[2048]{0:T(1024)S(1)}, f32[2048]{0:T(1024)S(1)}, f32[2048]{0:T(1024)S(1)}, bf16[2048,2048]{1,0:T(8,128)(2,1)}, /*index=5*/bf16[2048,2048]{1,0:T(8,128)(2,1)}) fusion(bf16[2048,2048]{1,0:T(8,128)(2,1)} %copy-done.4, f32[2048]{0:T(1024)S(1)} %copy-done.51, f32[2048]{0:T(1024)S(1)} %copy-done.49, ...), kind=kOutput, calls=%fused_computation.10 | convolution fusion | flops 6509551616 | bytes 48308224 | tf_op jit(solution)/shard_map/dot_general | solution.py:17
  487.6 8.1 add_convert_fusion.1
  502.0 7.3 fusion.63
  530.0 12.2 %collective-permute-done.42 = bf16[256,512]{1,0:T(8,128)(2,1)S(1)} collective-permute-done((bf16[256,512]{1,0:T(8,128)(2,1)S(1)}, bf16[256,512]{1,0:T(8,128)(2,1)S(1)}, u32[]{:S(2)}, u32[]{:S(2)}) %collective-permute-start.42) | collective-permute-done | bytes 262176 | tf_op jit(solution)/shard_map/ppermute | solution.py:145
  548.4 7.3 convert_add_fusion.6
  567.9 24.0 %collective-permute-done.47 = bf16[1024,1024]{1,0:T(8,128)(2,1)} collective-permute-done((bf16[1024,1024]{1,0:T(8,128)(2,1)}, bf16[1024,1024]{1,0:T(8,128)(2,1)}, u32[]{:S(2)}, u32[]{:S(2)}) %collective-permute-start.47) | collective-permute-done | bytes 2097184 | tf_op jit(solution)/shard_map/ppermute | solution.py:145
  593.4 8.7 %convert_add_fusion.2 = f32[1024,1024]{1,0:T(8,128)S(1)} fusion(bf16[1024,1024]{1,0:T(8,128)(2,1)} %collective-permute-done.47, bf16[2048,1024]{1,0:T(8,128)(2,1)} %get-tuple-element.147, bf16[2048,256]{1,0:T(8,128)(2,1)} %get-tuple-element.76, bf16[2048,256]{1,0:T(8,128)(2,1)} %get-tuple-element.78, bf16[2048,256]{1,0:T(8,128)(2,1)S(1)} %copy-done.36, ...), kind=kOutput, calls=%fused_computation.99 | convolution fusion | flops 4313841664 | bytes 14680064 | tf_op jit(solution)/shard_map/dot_general | solution.py:17
  602.1 8.1 collective-permute-done.21
  614.0 39.2 %collective-permute-done.29 = bf16[2,256,2048]{2,1,0:T(8,128)(2,1)} collective-permute-done((bf16[2,256,2048]{2,1,0:T(8,128)(2,1)S(1)}, bf16[2,256,2048]{2,1,0:T(8,128)(2,1)}, u32[]{:S(2)}, u32[]{:S(2)}) %collective-permute-start.29) | collective-permute-done | bytes 2097184 | tf_op jit(solution)/shard_map/ppermute | solution.py:148
  660.6 7.7 convert_add_fusion.3
  673.9 28.0 %collective-permute-done.22 = bf16[256,2048]{1,0:T(8,128)(2,1)S(1)} collective-permute-done((bf16[256,2048]{1,0:T(8,128)(2,1)S(1)}, bf16[256,2048]{1,0:T(8,128)(2,1)S(1)}, u32[]{:S(2)}, u32[]{:S(2)}) %collective-permute-start.22) | collective-permute-done | bytes 1048608 | tf_op jit(solution)/shard_map/ppermute | solution.py:145
  706.8 7.8 rev.7
  724.9 7.8 rev.8
  745.5 19.3 %collective-permute-done.45 = bf16[512,1024]{0,1:T(8,128)(2,1)S(1)} collective-permute-done((bf16[512,1024]{0,1:T(8,128)(2,1)}, bf16[512,1024]{0,1:T(8,128)(2,1)S(1)}, u32[]{:S(2)}, u32[]{:S(2)}) %collective-permute-start.45) | collective-permute-done | bytes 1048608 | tf_op jit(solution)/shard_map/ppermute | solution.py:145
  773.0 16.9 %collective-permute-done.23 = bf16[256,2048]{1,0:T(8,128)(2,1)S(1)} collective-permute-done((bf16[256,2048]{1,0:T(8,128)(2,1)S(1)}, bf16[256,2048]{1,0:T(8,128)(2,1)S(1)}, u32[]{:S(2)}, u32[]{:S(2)}) %collective-permute-start.23) | collective-permute-done | bytes 1048608 | tf_op jit(solution)/shard_map/ppermute | solution.py:148
  813.9 17.4 %collective-permute-done.49 = f32[1024,256]{1,0:T(8,128)} collective-permute-done((f32[1024,256]{1,0:T(8,128)}, f32[1024,256]{1,0:T(8,128)}, u32[]{:S(2)}, u32[]{:S(2)}) %collective-permute-start.49) | collective-permute-done | bytes 1048608 | tf_op jit(solution)/shard_map/ppermute | solution.py:145
  (514 shorter events, 333.9 us)
Async XLA Ops:
  3.3 125.9 %collective-permute-start.25 = (bf16[256,2048]{1,0:T(8,128)(2,1)}, bf16[256,2048]{1,0:T(8,128)(2,1)}, u32[]{:S(2)}, u32[]{:S(2)}) collective-permute-start(bf16[256,2048]{1,0:T(8,128)(2,1)} %dynamic-slice_bitcast_fusion), channel_id=1, source_target_pairs={{0,8},{4,12},{8,0},{12,4},{16,24},{20,28},{24,16},{28,20},{1,9},{5... | collective-permute-start | bytes 3145736 | tf_op jit(solution)/shard_map/ppermute | solution.py:145
  8.8 94.9 %collective-permute-start = (bf16[256,2048]{1,0:T(8,128)(2,1)}, bf16[256,2048]{1,0:T(8,128)(2,1)}, u32[]{:S(2)}, u32[]{:S(2)}) collective-permute-start(bf16[256,2048]{1,0:T(8,128)(2,1)} %dynamic-slice_bitcast_fusion.1), channel_id=1, source_target_pairs={{0,8},{4,12},{8,0},{12,4},{16,24},{20,28},{24,16},{28,20},{1,9},{5... | collective-permute-start | bytes 3145736 | tf_op jit(solution)/shard_map/ppermute | solution.py:145
  11.3 92.3 %collective-permute-start.3 = (bf16[256,1,768]{2,0,1:T(8,128)(2,1)}, bf16[256,1,768]{2,0,1:T(8,128)(2,1)S(1)}, u32[]{:S(2)}, u32[]{:S(2)}) collective-permute-start(bf16[256,1,768]{2,0,1:T(8,128)(2,1)} %copy.59), channel_id=1, source_target_pairs={{0,8},{4,12},{8,0},{12,4},{16,24},{20,28},{24,16},{28,20},{1,9},{5... | collective-permute-start | bytes 1179656 | tf_op jit(solution)/shard_map/ppermute | solution.py:145
  13.3 76.3 %collective-permute-start.7 = (s32[1024]{0:T(1024)S(1)}, s32[1024]{0:T(1024)}, u32[]{:S(2)}, u32[]{:S(2)}) collective-permute-start(s32[1024]{0:T(1024)S(1)} %bitcast.158), channel_id=1, source_target_pairs={{0,8},{4,12},{8,0},{12,4},{16,24},{20,28},{24,16},{28,20},{1,9},{5... | collective-permute-start | bytes 12296 | tf_op jit(solution)/shard_map/ppermute | solution.py:145
  15.2 69.9 %collective-permute-start.8 = (bf16[256,256]{1,0:T(8,128)(2,1)}, bf16[256,256]{1,0:T(8,128)(2,1)}, u32[]{:S(2)}, u32[]{:S(2)}) collective-permute-start(bf16[256,256]{1,0:T(8,128)(2,1)} %get-tuple-element.123), channel_id=1, source_target_pairs={{0,8},{4,12},{8,0},{12,4},{16,24},{20,28},{24,16},{28,20},{1,9},{5... | collective-permute-start | bytes 393224 | tf_op jit(solution)/shard_map/ppermute | solution.py:145
  103.7 77.9 %collective-permute-start.1 = (bf16[256,2048]{1,0:T(8,128)(2,1)}, bf16[256,2048]{1,0:T(8,128)(2,1)}, u32[]{:S(2)}, u32[]{:S(2)}) collective-permute-start(bf16[256,2048]{1,0:T(8,128)(2,1)} %collective-permute-done), channel_id=1, source_target_pairs={{0,2},{1,3},{2,0},{3,1},{4,6},{5,7},{6,4},{7,5},{8,10},{9,11},{10,... | collective-permute-start | bytes 3145736 | tf_op jit(solution)/shard_map/ppermute | solution.py:148
  108.6 72.3 %collective-permute-start.4 = (bf16[512,1,768]{2,0,1:T(8,128)(2,1)}, bf16[512,1,768]{2,0,1:T(8,128)(2,1)}, u32[]{:S(2)}, u32[]{:S(2)}) collective-permute-start(bf16[512,1,768]{2,0,1:T(8,128)(2,1)} %pad_maximum_fusion.4), channel_id=1, source_target_pairs={{0,16},{4,20},{8,24},{12,28},{16,0},{20,4},{24,8},{28,12},{1,17},{... | collective-permute-start | bytes 2359304 | tf_op jit(solution)/shard_map/ppermute | solution.py:145
  124.3 62.0 %collective-permute-start.5 = (bf16[512,1,768]{2,0,1:T(8,128)(2,1)}, bf16[512,1,768]{2,0,1:T(8,128)(2,1)S(1)}, u32[]{:S(2)}, u32[]{:S(2)}) collective-permute-start(bf16[512,1,768]{2,0,1:T(8,128)(2,1)} %pad_maximum_fusion.4), channel_id=1, source_target_pairs={{0,4},{4,0},{8,12},{12,8},{16,20},{20,16},{24,28},{28,24},{1,5},{5... | collective-permute-start | bytes 2359304 | tf_op jit(solution)/shard_map/ppermute | solution.py:145
  125.8 88.7 %collective-permute-start.13 = (bf16[512,1024]{1,0:T(8,128)(2,1)S(1)}, bf16[512,1024]{1,0:T(8,128)(2,1)S(1)}, u32[]{:S(2)}, u32[]{:S(2)}) collective-permute-start(bf16[512,1024]{1,0:T(8,128)(2,1)S(1)} %pad_maximum_fusion.2), channel_id=1, source_target_pairs={{0,16},{4,20},{8,24},{12,28},{16,0},{20,4},{24,8},{28,12},{1,17},{... | collective-permute-start | bytes 3145736 | tf_op jit(solution)/shard_map/ppermute | solution.py:145
  129.2 88.5 %collective-permute-start.14 = (bf16[512,1024]{1,0:T(8,128)(2,1)S(1)}, bf16[512,1024]{1,0:T(8,128)(2,1)S(1)}, u32[]{:S(2)}, u32[]{:S(2)}) collective-permute-start(bf16[512,1024]{1,0:T(8,128)(2,1)S(1)} %pad_maximum_fusion.2), channel_id=1, source_target_pairs={{0,4},{4,0},{8,12},{12,8},{16,20},{20,16},{24,28},{28,24},{1,5},{5... | collective-permute-start | bytes 3145736 | tf_op jit(solution)/shard_map/ppermute | solution.py:145
  180.9 54.2 %collective-permute-start.17 = (bf16[1024,512]{1,0:T(8,128)(2,1)S(1)}, bf16[1024,512]{1,0:T(8,128)(2,1)S(1)}, u32[]{:S(2)}, u32[]{:S(2)}) collective-permute-start(bf16[1024,512]{1,0:T(8,128)(2,1)S(1)} %pad_maximum_fusion.3), channel_id=1, source_target_pairs={{0,16},{4,20},{8,24},{12,28},{16,0},{20,4},{24,8},{28,12},{1,17},{... | collective-permute-start | bytes 3145736 | tf_op jit(solution)/shard_map/ppermute | solution.py:145
  181.6 55.1 %collective-permute-start.18 = (bf16[1024,512]{1,0:T(8,128)(2,1)S(1)}, bf16[1024,512]{1,0:T(8,128)(2,1)S(1)}, u32[]{:S(2)}, u32[]{:S(2)}) collective-permute-start(bf16[1024,512]{1,0:T(8,128)(2,1)S(1)} %pad_maximum_fusion.3), channel_id=1, source_target_pairs={{0,4},{4,0},{8,12},{12,8},{16,20},{20,16},{24,28},{28,24},{1,5},{5... | collective-permute-start | bytes 3145736 | tf_op jit(solution)/shard_map/ppermute | solution.py:145
  186.3 94.7 %collective-permute-start.2 = (bf16[512,2048]{1,0:T(8,128)(2,1)S(1)}, bf16[512,2048]{1,0:T(8,128)(2,1)S(1)}, u32[]{:S(2)}, u32[]{:S(2)}) collective-permute-start(bf16[512,2048]{1,0:T(8,128)(2,1)S(1)} %maximum_select_fusion.4), channel_id=1, source_target_pairs={{0,1},{1,0},{2,3},{3,2},{4,5},{5,4},{6,7},{7,6},{8,9},{9,8},{10,11... | collective-permute-start | bytes 6291464 | tf_op jit(solution)/shard_map/ppermute | solution.py:148
  236.7 44.1 %collective-permute-start.19 = (bf16[1024,512]{1,0:T(8,128)(2,1)S(1)}, bf16[1024,512]{1,0:T(8,128)(2,1)S(1)}, u32[]{:S(2)}, u32[]{:S(2)}) collective-permute-start(bf16[1024,512]{1,0:T(8,128)(2,1)S(1)} %collective-permute-done.17), channel_id=1, source_target_pairs={{0,4},{4,0},{8,12},{12,8},{16,20},{20,16},{24,28},{28,24},{1,5},{5... | collective-permute-start | bytes 3145736 | tf_op jit(solution)/shard_map/ppermute | solution.py:145
  241.2 62.5 %collective-permute-start.27 = (bf16[512,2048]{1,0:T(8,128)(2,1)S(1)}, bf16[512,2048]{1,0:T(8,128)(2,1)}, u32[]{:S(2)}, u32[]{:S(2)}) collective-permute-start(bf16[512,2048]{1,0:T(8,128)(2,1)S(1)} %maximum_select_fusion.6), channel_id=1, source_target_pairs={{0,1},{1,0},{2,3},{3,2},{4,5},{5,4},{6,7},{7,6},{8,9},{9,8},{10,11... | collective-permute-start | bytes 6291464 | tf_op jit(solution)/shard_map/ppermute | solution.py:148
  444.9 80.2 %collective-permute-start.41 = (bf16[256,1024]{1,0:T(8,128)(2,1)}, bf16[256,1024]{1,0:T(8,128)(2,1)}, u32[]{:S(2)}, u32[]{:S(2)}) collective-permute-start(bf16[256,1024]{1,0:T(8,128)(2,1)} %convolution_convert_fusion.2), channel_id=1, source_target_pairs={{0,4},{4,0},{8,12},{12,8},{16,20},{20,16},{24,28},{28,24},{1,5},{5... | collective-permute-start | bytes 1572872 | tf_op jit(solution)/shard_map/ppermute | solution.py:145
  502.0 54.9 %collective-permute-start.20 = (bf16[2,512,2048]{2,1,0:T(8,128)(2,1)}, bf16[2,512,2048]{2,1,0:T(8,128)(2,1)}, u32[]{:S(2)}, u32[]{:S(2)}) collective-permute-start(bf16[2,512,2048]{2,1,0:T(8,128)(2,1)} %constant_dynamic-slice_fusion.9), channel_id=1, source_target_pairs={{0,1},{1,0},{2,3},{3,2},{4,5},{5,4},{6,7},{7,6},{8,9},{9,8},{10,11... | collective-permute-start | bytes 12582920 | tf_op jit(solution)/shard_map/ppermute | solution.py:148
  513.8 47.7 %collective-permute-start.28 = (bf16[2,512,2048]{2,1,0:T(8,128)(2,1)}, bf16[2,512,2048]{2,1,0:T(8,128)(2,1)}, u32[]{:S(2)}, u32[]{:S(2)}) collective-permute-start(bf16[2,512,2048]{2,1,0:T(8,128)(2,1)} %constant_dynamic-slice_fusion.8), channel_id=1, source_target_pairs={{0,1},{1,0},{2,3},{3,2},{4,5},{5,4},{6,7},{7,6},{8,9},{9,8},{10,11... | collective-permute-start | bytes 12582920 | tf_op jit(solution)/shard_map/ppermute | solution.py:148
  529.8 62.0 %collective-permute-start.47 = (bf16[1024,1024]{1,0:T(8,128)(2,1)}, bf16[1024,1024]{1,0:T(8,128)(2,1)}, u32[]{:S(2)}, u32[]{:S(2)}) collective-permute-start(bf16[1024,1024]{1,0:T(8,128)(2,1)} %convolution_convert_fusion.1), channel_id=1, source_target_pairs={{0,4},{4,0},{8,12},{12,8},{16,20},{20,16},{24,28},{28,24},{1,5},{5... | collective-permute-start | bytes 6291464 | tf_op jit(solution)/shard_map/ppermute | solution.py:145
  542.1 118.1 %collective-permute-start.44 = (bf16[1024,1024]{0,1:T(8,128)(2,1)}, bf16[1024,1024]{0,1:T(8,128)(2,1)}, u32[]{:S(2)}, u32[]{:S(2)}) collective-permute-start(bf16[1024,1024]{0,1:T(8,128)(2,1)} %fusion.60), channel_id=1, source_target_pairs={{0,4},{4,0},{8,12},{12,8},{16,20},{20,16},{24,28},{28,24},{1,5},{5... | collective-permute-start | bytes 6291464 | tf_op jit(solution)/shard_map/ppermute | solution.py:145
  546.9 245.3 %collective-permute-start.37 = (f32[8192]{0:T(1024)S(1)}, f32[8192]{0:T(1024)S(1)}, u32[]{:S(2)}, u32[]{:S(2)}) collective-permute-start(f32[8192]{0:T(1024)S(1)} %slice_add_fusion.4), channel_id=1, source_target_pairs={{0,2},{1,3},{2,0},{3,1},{4,6},{5,7},{6,4},{7,5},{8,10},{9,11},{10,... | collective-permute-start | bytes 98312 | tf_op jit(solution)/shard_map/ppermute | solution.py:148
  557.6 236.5 %collective-permute-start.43 = (f32[256,256]{1,0:T(8,128)}, f32[256,256]{1,0:T(8,128)}, u32[]{:S(2)}, u32[]{:S(2)}) collective-permute-start(f32[256,256]{1,0:T(8,128)} %get-tuple-element.122), channel_id=1, source_target_pairs={{0,8},{4,12},{8,0},{12,4},{16,24},{20,28},{24,16},{28,20},{1,9},{5... | collective-permute-start | bytes 786440 | tf_op jit(solution)/shard_map/ppermute | solution.py:145
  561.6 48.6 %collective-permute-start.21 = (bf16[2,256,2048]{2,1,0:T(8,128)(2,1)S(1)}, bf16[2,256,2048]{2,1,0:T(8,128)(2,1)S(1)}, u32[]{:S(2)}, u32[]{:S(2)}) collective-permute-start(bf16[2,256,2048]{2,1,0:T(8,128)(2,1)S(1)} %dynamic-slice_convert_fusion.1), channel_id=1, source_target_pairs={{0,2},{1,3},{2,0},{3,1},{4,6},{5,7},{6,4},{7,5},{8,10},{9,11},{10,... | collective-permute-start | bytes 6291464 | tf_op jit(solution)/shard_map/ppermute | solution.py:148
  591.8 61.4 %collective-permute-start.29 = (bf16[2,256,2048]{2,1,0:T(8,128)(2,1)S(1)}, bf16[2,256,2048]{2,1,0:T(8,128)(2,1)}, u32[]{:S(2)}, u32[]{:S(2)}) collective-permute-start(bf16[2,256,2048]{2,1,0:T(8,128)(2,1)S(1)} %dynamic-slice_convert_fusion), channel_id=1, source_target_pairs={{0,2},{1,3},{2,0},{3,1},{4,6},{5,7},{6,4},{7,5},{8,10},{9,11},{10,... | collective-permute-start | bytes 6291464 | tf_op jit(solution)/shard_map/ppermute | solution.py:148
  611.5 59.1 %collective-permute-start.39 = (bf16[512,768]{0,1:T(8,128)(2,1)}, bf16[512,768]{0,1:T(8,128)(2,1)S(1)}, u32[]{:S(2)}, u32[]{:S(2)}) collective-permute-start(bf16[512,768]{0,1:T(8,128)(2,1)} %split.94), channel_id=1, source_target_pairs={{0,16},{4,20},{8,24},{12,28},{16,0},{20,4},{24,8},{28,12},{1,17},{... | collective-permute-start | bytes 2359304 | tf_op jit(solution)/shard_map/ppermute | solution.py:145
  653.3 48.7 %collective-permute-start.22 = (bf16[256,2048]{1,0:T(8,128)(2,1)S(1)}, bf16[256,2048]{1,0:T(8,128)(2,1)S(1)}, u32[]{:S(2)}, u32[]{:S(2)}) collective-permute-start(bf16[256,2048]{1,0:T(8,128)(2,1)S(1)} %fusion.82), channel_id=1, source_target_pairs={{0,8},{4,12},{8,0},{12,4},{16,24},{20,28},{24,16},{28,20},{1,9},{5... | collective-permute-start | bytes 3145736 | tf_op jit(solution)/shard_map/ppermute | solution.py:145
  660.3 61.3 %collective-permute-start.30 = (bf16[256,2048]{1,0:T(8,128)(2,1)}, bf16[256,2048]{1,0:T(8,128)(2,1)}, u32[]{:S(2)}, u32[]{:S(2)}) collective-permute-start(bf16[256,2048]{1,0:T(8,128)(2,1)} %fusion.83), channel_id=1, source_target_pairs={{0,8},{4,12},{8,0},{12,4},{16,24},{20,28},{24,16},{28,20},{1,9},{5... | collective-permute-start | bytes 3145736 | tf_op jit(solution)/shard_map/ppermute | solution.py:145
  670.6 96.3 %collective-permute-start.48 = (bf16[1024,512]{1,0:T(8,128)(2,1)}, bf16[1024,512]{1,0:T(8,128)(2,1)}, u32[]{:S(2)}, u32[]{:S(2)}) collective-permute-start(bf16[1024,512]{1,0:T(8,128)(2,1)} %split.92), channel_id=1, source_target_pairs={{0,16},{4,20},{8,24},{12,28},{16,0},{20,4},{24,8},{28,12},{1,17},{... | collective-permute-start | bytes 3145736 | tf_op jit(solution)/shard_map/ppermute | solution.py:145
  702.9 61.9 %collective-permute-start.45 = (bf16[512,1024]{0,1:T(8,128)(2,1)}, bf16[512,1024]{0,1:T(8,128)(2,1)S(1)}, u32[]{:S(2)}, u32[]{:S(2)}) collective-permute-start(bf16[512,1024]{0,1:T(8,128)(2,1)} %split.93), channel_id=1, source_target_pairs={{0,16},{4,20},{8,24},{12,28},{16,0},{20,4},{24,8},{28,12},{1,17},{... | collective-permute-start | bytes 3145736 | tf_op jit(solution)/shard_map/ppermute | solution.py:145
  768.5 41.6 %collective-permute-start.46 = (f32[256,1024]{0,1:T(8,128)}, f32[256,1024]{0,1:T(8,128)}, u32[]{:S(2)}, u32[]{:S(2)}) collective-permute-start(f32[256,1024]{0,1:T(8,128)} %get-tuple-element.112), channel_id=1, source_target_pairs={{0,8},{4,12},{8,0},{12,4},{16,24},{20,28},{24,16},{28,20},{1,9},{5... | collective-permute-start | bytes 3145736 | tf_op jit(solution)/shard_map/ppermute | solution.py:145
  789.9 44.7 %collective-permute-start.32 = (bf16[512,2048]{1,0:T(8,128)(2,1)}, bf16[512,2048]{1,0:T(8,128)(2,1)}, u32[]{:S(2)}, u32[]{:S(2)}) collective-permute-start(bf16[512,2048]{1,0:T(8,128)(2,1)} %maximum_select_fusion.7), channel_id=1, source_target_pairs={{0,1},{1,0},{2,3},{3,2},{4,5},{5,4},{6,7},{7,6},{8,9},{9,8},{10,11... | collective-permute-start | bytes 6291464 | tf_op jit(solution)/shard_map/ppermute | solution.py:148
  792.2 48.4 %collective-permute-start.24 = (bf16[512,2048]{1,0:T(8,128)(2,1)}, bf16[512,2048]{1,0:T(8,128)(2,1)}, u32[]{:S(2)}, u32[]{:S(2)}) collective-permute-start(bf16[512,2048]{1,0:T(8,128)(2,1)} %maximum_select_fusion.5), channel_id=1, source_target_pairs={{0,1},{1,0},{2,3},{3,2},{4,5},{5,4},{6,7},{7,6},{8,9},{9,8},{10,11... | collective-permute-start | bytes 6291464 | tf_op jit(solution)/shard_map/ppermute | solution.py:148
  (112 other events, 2098.1 us)

commit v2 on v1

--- a/solution.py
+++ b/solution.py
@@ -1,3 +1,5 @@
+import functools
+
 import jax
 import jax.numpy as jnp
 from jax import lax
@@ -103,15 +105,472 @@
         sum_ref[0, :, number * size : (number + 1) * size] = jnp.sum(part.astype(F), axis=0, keepdims=True)
 
 
+def pre_kernel(g_ref, w_ref, slope_ref, out_ref, sum_ref):
+    grad = (dot(g_ref[...], w_ref[...], ((1,), (0,)), F) * slope_ref[...]).astype(B)
+    out_ref[...] = grad
+
+    @pl.when(pl.program_id(0) == 0)
+    def _():
+        sum_ref[...] = jnp.zeros_like(sum_ref)
+
+    sum_ref[...] += jnp.sum(grad.astype(F), axis=0, keepdims=True)
+
+
+def branch_kernel(ctx_ref, act_ref, dense_ref, down_ref, out_ref):
+    width = out_ref.shape[1]
+    for low in range(0, width, 512):
+        here = slice(low, low + 512)
+        out_ref[:, here] = (
+            dot(ctx_ref[...], dense_ref[here, :], ((1,), (1,)), F)
+            + dot(act_ref[...], down_ref[here, :], ((1,), (1,)), F)
+        ).astype(B)
+
+
+def blend_kernel(part, order_ref, mixed_ref, pre_ref, qkv_ref, up_ref, x_ref, vec_ref, out_ref, sum_ref):
+    @pl.when(pl.program_id(0) == 0)
+    def _():
+        sum_ref[...] = jnp.zeros_like(sum_ref)
+
+    rows = x_ref[...].astype(F)
+    mean = jnp.mean(rows, axis=1, keepdims=True)
+    center = rows - mean
+    inverse = lax.rsqrt(jnp.mean(center * center, axis=1, keepdims=True) + 1e-05)
+    for place in range(x_ref.shape[1] // part):
+        here = slice(place * part, (place + 1) * part)
+        there = pl.ds(pl.multiple_of(order_ref[place] * part, part), part)
+        attn_grad = dot(mixed_ref[...], qkv_ref[here, :], ((1,), (1,)), F)
+        mlp_grad = dot(pre_ref[...], up_ref[here, :], ((1,), (1,)), F)
+        normed = (x_ref[:, here].astype(F) - mean) * inverse
+        out_ref[:, here] = (attn_grad * vec_ref[0:1, there] + mlp_grad * vec_ref[2:3, there]).astype(B)
+        sum_ref[0:1, there] += jnp.sum(attn_grad * normed, axis=0, keepdims=True)
+        sum_ref[1:2, there] += jnp.sum(attn_grad, axis=0, keepdims=True)
+        sum_ref[2:3, there] += jnp.sum(mlp_grad * normed, axis=0, keepdims=True)
+        sum_ref[3:4, there] += jnp.sum(mlp_grad, axis=0, keepdims=True)
+
+
+def finish_out(part, place_ref, held_ref, sent_ref, x_ref, vec_ref, out_ref):
+    for block in range(x_ref.shape[1] // part):
+        here = slice(block * part, (block + 1) * part)
+        place, other = place_ref[0, block], place_ref[1, block]
+        mine = held_ref[:, pl.ds(pl.multiple_of(place * part, part), part)]
+        theirs = sent_ref[:, pl.ds(pl.multiple_of(other * part, part), part)].astype(F)
+        bias = vec_ref[4:5, here] + vec_ref[5:6, here]
+        out_ref[:, here] = (x_ref[:, here].astype(F) + (mine + theirs) + bias).astype(B)
+
+
+def finish_grad(part, place_ref, held_ref, sent_ref, x_ref, g_ref, out_ref):
+    rows = x_ref[...].astype(F)
+    mean = jnp.mean(rows, axis=1, keepdims=True)
+    center = rows - mean
+    inverse = lax.rsqrt(jnp.mean(center * center, axis=1, keepdims=True) + 1e-05)
+    blends = []
+    for block in range(x_ref.shape[1] // part):
+        place, other = place_ref[0, block], place_ref[1, block]
+        mine = held_ref[:, pl.ds(pl.multiple_of(place * part, part), part)]
+        theirs = sent_ref[:, pl.ds(pl.multiple_of(other * part, part), part)].astype(F)
+        blends.append(mine + theirs)
+    blend = jnp.concatenate(blends, axis=1)
+    normed = center * inverse
+    inner = blend - jnp.mean(blend, axis=1, keepdims=True) - normed * jnp.mean(blend * normed, axis=1, keepdims=True)
+    out_ref[...] = (g_ref[...].astype(F) + inner * inverse).astype(B)
+
+
 def per_seq(rows, columns):
-    return pl.BlockSpec((1, rows, columns), lambda seq: (seq, 0, 0))
+    return pl.BlockSpec((1, rows, columns), lambda seq, *_: (seq, 0, 0))
 
 
 def shared(rows, columns):
-    return pl.BlockSpec((rows, columns), lambda seq: (0, 0))
-
-
-def body(
+    return pl.BlockSpec((rows, columns), lambda *_: (0, 0))
+
+
+def tiled(rows, columns):
+    return pl.BlockSpec((rows, columns), lambda tile, *_: (tile, 0))
+
+
+def call(kernel, grid, in_specs, out_specs, out_shape, flops, moved, prefetch=0, aliases=None, scratch=(), name=None):
+    return pl.pallas_call(
+        kernel,
+        grid_spec=pltpu.PrefetchScalarGridSpec(
+            num_scalar_prefetch=prefetch, grid=grid, in_specs=in_specs, out_specs=out_specs, scratch_shapes=list(scratch)
+        ),
+        out_shape=out_shape,
+        input_output_aliases=aliases or {},
+        cost_estimate=pl.CostEstimate(flops=flops, bytes_accessed=moved, transcendentals=0),
+        compiler_params=pltpu.CompilerParams(vmem_limit_bytes=56 * 1024 * 1024),
+        name=name,
+    )
+
+
+MESH = pl.DeviceIdType.MESH
+CHUNK = 256
+
+
+def bit_of(index, bit):
+    return lax.rem(lax.div(index, bit), 2)
+
+
+def flip(index, mask):
+    bit = 1
+    while bit <= mask:
+        if mask & bit:
+            index = index + bit * (1 - 2 * bit_of(index, bit))
+        bit *= 2
+    return index
+
+
+def block_order(groups):
+    spread = [bit for bit in (1 << k for k in reversed(range(groups.bit_length() - 1))) if bit != PAIR]
+    order = [0, PAIR]
+    for bit in spread:
+        order = order + [mask | bit for mask in order]
+    return spread, order
+
+
+def stats(rows):
+    mean = jnp.mean(rows, axis=1, keepdims=True)
+    center = rows - mean
+    return mean, lax.rsqrt(jnp.mean(center * center, axis=1, keepdims=True) + 1e-05)
+
+
+def greet(partners):
+    barrier = pltpu.get_barrier_semaphore()
+    for axis, index in partners:
+        pl.semaphore_signal(barrier, inc=1, device_id={axis: index}, device_id_type=MESH)
+    pl.semaphore_wait(barrier, len(partners))
+
+
+def gather_kernel(
+    groups,
+    mine_ref,
+    theirs_ref,
+    x_ref,
+    g_ref,
+    vec_ref,
+    up_bias_ref,
+    offset_ref,
+    cos_ref,
+    above_ref,
+    below_ref,
+    col_ref,
+    row_ref,
+    w_out,
+    x_other,
+    g_other,
+    x_rel,
+    g_rel,
+    mlp_out,
+    mixed_out,
+    ctx_out,
+    act_out,
+    slope_out,
+    send_out,
+    keep_out,
+    sum_ref,
+    w,
+    raw_x,
+    raw_g,
+    attn_v,
+    g_v,
+    mlp_v,
+    xr_v,
+    grad_v,
+    send_v,
+    q_v,
+    k_v,
+    v_v,
+    cg_v,
+    ctx_v,
+    mg_v,
+    dk_v,
+    dv_v,
+    act_v,
+    slope_v,
+    send_sem,
+    recv_sem,
+    own_sem,
+    load_sem,
+    rel_sem,
+    tile_sem,
+    out_sem,
+):
+    length, width = x_ref.shape
+    part = width // groups
+    size = q_v.shape[1]
+    quarter = length // 4
+    me, place = lax.axis_index("dp"), lax.axis_index("tensor")
+    core, side = lax.rem(place, 2), lax.div(place, 2)
+    pair_to, side_to, core_to = flip(me, PAIR), flip(place, 2), flip(place, 1)
+    spread, order = block_order(groups)
+    greet([("dp", flip(me, bit)) for bit in [PAIR] + spread] + [("tensor", side_to), ("tensor", core_to)])
+    copies = {}
+
+    def remote(key, source, target, axis, index):
+        number = len(copies)
+        copies[key] = pltpu.make_async_remote_copy(
+            src_ref=source,
+            dst_ref=target,
+            send_sem=send_sem.at[number],
+            recv_sem=recv_sem.at[number],
+            device_id={axis: index},
+            device_id_type=MESH,
+        )
+        copies[key].start()
+
+    def rows(position):
+        return pl.ds(position * part, part)
+
+    def pair_up(group):
+        remote(("w", group, 1), theirs_ref.at[group], w.at[group, rows(1)], "dp", pair_to)
+
+    def onward(group, position, level):
+        source = mine_ref.at[group] if position == 0 else w.at[group, rows(position)]
+        far = position + (2 << level)
+        remote(("w", group, far), source, w.at[group, rows(far)], "dp", flip(me, spread[level]))
+
+    def arrive(group, position, ahead=()):
+        copies[("w", group, position)].wait_recv()
+
+    spot = pl.ds(pl.multiple_of(core * (2 * quarter) + side * quarter, quarter), quarter)
+    pair_rows = pl.ds(pl.multiple_of(core * (2 * quarter), quarter), 2 * quarter)
+    levels = len(spread)
+    assert levels == 2
+
+    def load(x, g, tile, slot):
+        here = pl.ds(pl.multiple_of(tile * CHUNK, CHUNK), CHUNK)
+        return (
+            pltpu.make_async_copy(x.at[here], raw_x.at[slot], load_sem.at[0, slot]),
+            pltpu.make_async_copy(g.at[here], raw_g.at[slot], load_sem.at[1, slot]),
+        )
+
+    def normalise(seq, x, g):
+        for copy in load(x, g, 0, 0):
+            copy.start()
+
+        def one(tile, carry):
+            slot = lax.rem(tile, 2)
+
+            @pl.when(tile + 1 < length // CHUNK)
+            def _():
+                for copy in load(x, g, tile + 1, 1 - slot):
+                    copy.start()
+
+            for copy in load(x, g, tile, slot):
+                copy.wait()
+            here = pl.ds(pl.multiple_of(tile * CHUNK, CHUNK), CHUNK)
+            both = pl.ds(pl.multiple_of(seq * length + tile * CHUNK, CHUNK), CHUNK)
+            mean, inverse = stats(raw_x[slot].astype(F))
+            for position, mask in enumerate(order):
+                to = slice(position * part, (position + 1) * part)
+                there = pl.ds(pl.multiple_of(flip(me, mask) * part, part), part)
+                piece = raw_x[slot, :, there]
+                normed = (piece.astype(F) - mean) * inverse
+                attn_v[here, to] = (normed * vec_ref[0:1, there] + vec_ref[1:2, there]).astype(B)
+                mlp_v[both, to] = (normed * vec_ref[2:3, there] + vec_ref[3:4, there]).astype(B)
+                xr_v[here, to] = piece
+                g_v[here, to] = raw_g[slot, :, there]
+            return carry
+
+        lax.fori_loop(0, length // CHUNK, one, 0)
+        both = pl.ds(seq * length, length)
+        return [
+            pltpu.make_async_copy(xr_v, x_rel.at[both], rel_sem.at[seq, 0]),
+            pltpu.make_async_copy(g_v, g_rel.at[both], rel_sem.at[seq, 1]),
+            pltpu.make_async_copy(mlp_v.at[both], mlp_out.at[both], rel_sem.at[seq, 2]),
+        ]
+
+    def project():
+        def one(tile, carry):
+            here = pl.ds(pl.multiple_of(tile * CHUNK, CHUNK), CHUNK)
+            mixed = dot(attn_v[here], w[0, :, : 3 * size], ((1,), (0,)), F) + offset_ref[...]
+            tables = (cos_ref[here], above_ref[here], below_ref[here])
+            q_v[here] = turn(mixed[:, :size], *tables).astype(B)
+            k_v[here] = turn(mixed[:, size : 2 * size], *tables).astype(B)
+            v_v[here] = mixed[:, 2 * size :].astype(B)
+            cg_v[here] = dot(g_v[here], w[0, :, 3 * size :], ((1,), (0,)), B)
+            return carry
+
+        lax.fori_loop(0, length // CHUNK, one, 0)
+
+    def attend(seq):
+        scale = size ** (-0.5)
+        dk_v[...] = jnp.zeros_like(dk_v)
+        dv_v[...] = jnp.zeros_like(dv_v)
+        for first in range(0, length, QBLOCK):
+            low, high = key_range(first)
+            here, keys = slice(first, first + QBLOCK), slice(low, high)
+            scores = dot(q_v[here], k_v[keys], ((1,), (1,)), F) * scale
+            row_ids = first + lax.broadcasted_iota(jnp.int32, (QBLOCK, high - low), 0)
+            key_ids = low + lax.broadcasted_iota(jnp.int32, (QBLOCK, high - low), 1)
+            allowed = (key_ids <= row_ids) & (col_ref[seq, here, :] == row_ref[seq, :, keys])
+            scores = jnp.where(allowed, scores, -1e30)
+            expo = jnp.exp(scores - jnp.max(scores, axis=1, keepdims=True))
+            probs = expo / jnp.sum(expo, axis=1, keepdims=True)
+            low_probs = probs.astype(B)
+            ctx_v[here] = dot(low_probs, v_v[keys], ((1,), (0,)), B)
+            dv_v[keys] += dot(low_probs, cg_v[here], ((0,), (0,)), F)
+            prob_grad = dot(cg_v[here], v_v[keys], ((1,), (1,)), F)
+            centred = jnp.sum(probs * prob_grad, axis=1, keepdims=True)
+            score_grad = (probs * (prob_grad - centred)).astype(B)
+            q_grad = dot(score_grad, k_v[keys], ((1,), (0,)), F) * scale
+            tables = (cos_ref[here], -above_ref[here], -below_ref[here])
+            mg_v[here, :size] = turn(q_grad, *tables).astype(B)
+            dk_v[keys] += dot(score_grad, q_v[here], ((0,), (0,)), F) * scale
+        for first in range(0, length, QBLOCK):
+            here = slice(first, first + QBLOCK)
+            tables = (cos_ref[here], -above_ref[here], -below_ref[here])
+            mg_v[here, size : 2 * size] = turn(dk_v[here], *tables).astype(B)
+            mg_v[here, 2 * size :] = dv_v[here].astype(B)
+        sums = jnp.sum(mg_v[...].astype(F), axis=0, keepdims=True)
+        if seq == 0:
+            sum_ref[...] = sums
+        else:
+            sum_ref[...] += sums
+        both = pl.ds(seq * length, length)
+        return [
+            pltpu.make_async_copy(mg_v, mixed_out.at[both], rel_sem.at[seq, 3]),
+            pltpu.make_async_copy(ctx_v, ctx_out.at[both], rel_sem.at[seq, 4]),
+        ]
+
+    def attn_grads(seq, low, high):
+        def one(block, carry):
+            here = pl.ds(pl.multiple_of(block * CHUNK, CHUNK), CHUNK)
+            qkv = dot(attn_v[:, here], mg_v[...], ((0,), (0,)), F)
+            dense = dot(g_v[:, here], ctx_v[...], ((0,), (0,)), F)
+            if seq == 0:
+                grad_v[here, : 3 * size] = qkv
+                grad_v[here, 3 * size :] = dense
+            else:
+                grad_v[here, : 3 * size] += qkv
+                grad_v[here, 3 * size :] += dense
+            return carry
+
+        lax.fori_loop(low // CHUNK, high // CHUNK, one, 0)
+
+    def up(low, high):
+        def store(tile, slot):
+            here = pl.ds(pl.multiple_of(tile * CHUNK, CHUNK), CHUNK)
+            return (
+                pltpu.make_async_copy(act_v.at[slot], act_out.at[here], tile_sem.at[0, slot]),
+                pltpu.make_async_copy(slope_v.at[slot], slope_out.at[here], tile_sem.at[1, slot]),
+            )
+
+        def one(tile, carry):
+            slot = lax.rem(tile, 2)
+            here = pl.ds(pl.multiple_of(tile * CHUNK, CHUNK), CHUNK)
+            pre = dot(mlp_v[here], w[1], ((1,), (0,)), F) + up_bias_ref[...]
+
+            @pl.when(tile >= low + 2)
+            def _():
+                for copy in store(tile - 2, slot):
+                    copy.wait()
+
+            cumulative = 0.5 * (1.0 + lax.erf(pre * 0.7071067811865476))
+            density = jnp.exp(-0.5 * pre * pre) * 0.3989422804014327
+            act_v[slot] = (pre * cumulative).astype(B)
+            slope_v[slot] = cumulative + pre * density
+            for copy in store(tile, slot):
+                copy.start()
+            return carry
+
+        lax.fori_loop(low, high, one, 0)
+        for tile in (high - 2, high - 1):
+            for copy in store(tile, tile % 2):
+                copy.wait()
+
+    def weights_out(group):
+        return pltpu.make_async_copy(w.at[group], w_out.at[group], out_sem.at[group])
+
+    pair_up(0)
+    onward(0, 0, 0)
+    onward(0, 0, 1)
+    own = [pltpu.make_async_copy(mine_ref.at[group], w.at[group, rows(0)], own_sem.at[group]) for group in range(3)]
+    for copy in own:
+        copy.start()
+    first_out = normalise(0, x_ref, g_ref)
+    for copy in first_out:
+        copy.start()
+    arrive(0, 1)
+    onward(0, 1, 0)
+    onward(0, 1, 1)
+    remote("x1", x_ref.at[spot], x_other.at[spot], "dp", pair_to)
+    pair_up(1)
+    onward(1, 0, 0)
+    onward(1, 0, 1)
+    arrive(0, 2)
+    onward(0, 2, 1)
+    remote("g1", g_ref.at[spot], g_other.at[spot], "dp", pair_to)
+    arrive(0, 3)
+    onward(0, 3, 1)
+    copies["x1"].wait_recv()
+    remote("x2", x_other.at[spot], x_other.at[spot], "tensor", side_to)
+    arrive(1, 1)
+    onward(1, 1, 0)
+    onward(1, 1, 1)
+    pair_up(2)
+    onward(2, 0, 0)
+    onward(2, 0, 1)
+    for position in range(4, 8):
+        arrive(0, position)
+    for copy in own:
+        copy.wait()
+    out = [weights_out(0)]
+    out[0].start()
+    project()
+    arrive(1, 2)
+    onward(1, 2, 1)
+    copies["x2"].wait_recv()
+    remote("x3", x_other.at[pair_rows], x_other.at[pair_rows], "tensor", core_to)
+    copies["g1"].wait_recv()
+    remote("g2", g_other.at[spot], g_other.at[spot], "tensor", side_to)
+    second_out = attend(0)
+    for copy in second_out:
+        copy.start()
+    arrive(2, 1)
+    onward(2, 1, 0)
+    onward(2, 1, 1)
+    arrive(1, 3)
+    onward(1, 3, 1)
+    attn_grads(0, 0, width)
+    copies["x3"].wait_recv()
+    copies["g2"].wait_recv()
+    remote("g3", g_other.at[pair_rows], g_other.at[pair_rows], "tensor", core_to)
+    for copy in first_out + second_out:
+        copy.wait()
+    copies["g3"].wait_recv()
+    arrive(2, 2)
+    onward(2, 2, 1)
+    third_out = normalise(1, x_other, g_other)
+    for copy in third_out:
+        copy.start()
+    project()
+    arrive(2, 3)
+    onward(2, 3, 1)
+    fourth_out = attend(1)
+    for copy in fourth_out:
+        copy.start()
+    attn_grads(1, width // 2, width)
+    send_v[...] = grad_v[width // 2 :].astype(B)
+    out.append(pltpu.make_async_copy(send_v, send_out, out_sem.at[3]))
+    out[-1].start()
+    attn_grads(1, 0, width // 2)
+    out.append(pltpu.make_async_copy(grad_v.at[pl.ds(0, width // 2)], keep_out, out_sem.at[4]))
+    out[-1].start()
+    for position in range(4, 8):
+        arrive(1, position)
+    out.append(weights_out(1))
+    out[-1].start()
+    up(0, 2 * length // CHUNK)
+    for position in range(4, 8):
+        arrive(2, position)
+    out.append(weights_out(2))
+    out[-1].start()
+    for copy in third_out + fourth_out + out:
+        copy.wait()
+    for copy in copies.values():
+        copy.wait_send()
+
+
+def body_narrow(
     tokens,
     segment_ids,
     out_grad,
@@ -357,6 +816,332 @@
     )
 
 
+def body(
+    tokens,
+    segment_ids,
+    out_grad,
+    attn_norm_gain,
+    attn_norm_bias,
+    mlp_norm_gain,
+    mlp_norm_bias,
+    qkv_weight,
+    qv_bias,
+    key_bias,
+    dense_weight,
+    dense_bias,
+    up_weight,
+    up_bias,
+    down_weight,
+    down_bias,
+    *,
+    groups,
+    ways,
+):
+    length, width = tokens.shape[1:]
+    heads, size = qkv_weight.shape[1] // 2, qkv_weight.shape[3]
+    assert heads == 1
+    part = width // groups
+    hidden = up_weight.shape[1] // 2
+    count = 2 * length
+    me = lax.axis_index("dp")
+    half = (me // PAIR) % 2
+    place = lax.axis_index("tensor")
+    core, side = place % 2, place // 2
+    spread = [bit for bit in (1 << k for k in reversed(range(groups.bit_length() - 1))) if bit != PAIR]
+    shape = jax.ShapeDtypeStruct
+    last = [me]
+
+    def swap(array, bit):
+        return lax.ppermute(array, "dp", [(i, i ^ bit) for i in range(groups)])
+
+    def cross(array, bit):
+        return lax.ppermute(array, "tensor", [(i, i ^ bit) for i in range(ways)])
+
+    def pick(array, index, axis, number=2):
+        rows = array.shape[axis] // number
+        return lax.dynamic_slice_in_dim(array, index * rows, rows, axis)
+
+    def join(mine, theirs, index, axis):
+        pair = jnp.concatenate([mine, theirs], axis=axis)
+        turned = jnp.concatenate([theirs, mine], axis=axis)
+        return jnp.where(index == 0, pair, turned)
+
+    def after(*values):
+        held, _ = lax.optimization_barrier((values, last[0]))
+        return held
+
+    def done(*values):
+        values = lax.optimization_barrier(values)
+        last[0] = values
+        return values
+
+    order = [0, PAIR]
+    for bit in spread:
+        order = order + [mask | bit for mask in order]
+    inverse = [order.index(mask) for mask in range(groups)]
+    held_at = jnp.asarray(inverse, jnp.int32)[jnp.arange(groups) ^ me]
+    place_table = jnp.stack([held_at, held_at ^ 1])
+    order_table = jnp.asarray(order, jnp.int32) ^ me
+    vectors = jnp.stack([attn_norm_gain, attn_norm_bias, mlp_norm_gain, mlp_norm_bias, dense_bias, down_bias])
+    step = part
+
+    def scatter(send, keep):
+        held = keep + swap(send, spread[-1]).astype(F)
+        for bit in reversed(spread[:-1]):
+            keep, send = jnp.split(held, 2, axis=0)
+            held = keep + swap(send.astype(B), bit).astype(F)
+        keep, send = jnp.split(held, 2, axis=0)
+        return keep, swap(send, PAIR)
+
+    def share_rows(rows):
+        pair = jnp.stack([rows, cross(rows, 2)])
+        quad = jnp.stack([pair, cross(pair, 1)])
+        quad = jnp.where(side == 0, quad, jnp.concatenate([quad[:, 1:], quad[:, :1]], axis=1))
+        quad = jnp.where(core == 0, quad, jnp.concatenate([quad[1:], quad[:1]], axis=0))
+        return quad.reshape(length, width)
+
+    def own_rows(array, axis):
+        return pick(pick(array, core, axis), side, axis)
+
+    def total_rows(partial):
+        partial = partial.reshape(2, length, width)
+        near = cross(pick(partial, 1 - core, 1), 1)
+        keep = pick(partial, core, 1)
+        far = (pick(keep, 1 - side, 1).astype(F) + pick(near, 1 - side, 1).astype(F)).astype(B)
+        far = cross(far, 2)
+        keep = pick(keep, side, 1).astype(F) + pick(near, side, 1).astype(F)
+        sent = swap((keep[1] + far[1].astype(F)).astype(B), PAIR)
+        return keep[0] + far[0].astype(F), sent
+
+    own_x, own_g = tokens[0], out_grad[0]
+
+    shards = [
+        jnp.concatenate(
+            [
+                qkv_weight.astype(B).reshape(part, 2, 3 * size),
+                dense_weight.astype(B).transpose(2, 0, 1),
+            ],
+            axis=2,
+        ),
+        up_weight.astype(B).reshape(part, 2, hidden),
+        down_weight.astype(B).reshape(2, hidden, part).transpose(2, 0, 1),
+    ]
+    mine = jnp.stack([pick(shard, half, 1)[:, 0] for shard in shards])
+    theirs = jnp.stack([pick(shard, 1 - half, 1)[:, 0] for shard in shards])
+
+    seg_other = swap(segment_ids[0], PAIR)
+    seg = jnp.stack([segment_ids[0], seg_other])
+    seg_col, seg_row = seg[:, :, None], seg[:, None, :]
+    qv_here, key_here = pick(qv_bias, half, 0), pick(key_bias, half, 0)
+    key_full = jnp.concatenate([key_here, jnp.zeros((heads, size - ROT), F)], axis=1)
+    offsets = jnp.stack([qv_here[:, 0], key_full, qv_here[:, 1]], axis=1).reshape(1, 3 * size)
+    tables = rope_tables(length)
+    up_here = pick(up_bias, half, 0)[None]
+    columns = hidden
+    half_width = width // 2
+    vmem, hbm = pl.BlockSpec(memory_space=pltpu.VMEM), pl.BlockSpec(memory_space=pl.ANY)
+    (
+        weights,
+        _,
+        _,
+        x_pair,
+        g_pair,
+        mlp_in,
+        mixed_grad,
+        context,
+        activation,
+        slope,
+        attn_send,
+        attn_keep,
+        mixed_sum,
+    ) = pl.pallas_call(
+        functools.partial(gather_kernel, groups),
+        in_specs=[hbm] * 4 + [vmem] * 8,
+        out_specs=[hbm] * 12 + [vmem],
+        out_shape=[
+            shape((3, width, columns), B),
+            shape((length, width), B),
+            shape((length, width), B),
+            shape((count, width), B),
+            shape((count, width), B),
+            shape((count, width), B),
+            shape((count, 3 * size), B),
+            shape((count, size), B),
+            shape((count, hidden), B),
+            shape((count, hidden), F),
+            shape((half_width, columns), B),
+            shape((half_width, columns), F),
+            shape((1, 3 * size), F),
+        ],
+        scratch_shapes=[
+            pltpu.VMEM((3, width, columns), B),
+            pltpu.VMEM((2, CHUNK, width), B),
+            pltpu.VMEM((2, CHUNK, width), B),
+            pltpu.VMEM((length, width), B),
+            pltpu.VMEM((length, width), B),
+            pltpu.VMEM((count, width), B),
+            pltpu.VMEM((length, width), B),
+            pltpu.VMEM((width, columns), F),
+            pltpu.VMEM((half_width, columns), B),
+            pltpu.VMEM((length, size), B),
+            pltpu.VMEM((length, size), B),
+            pltpu.VMEM((length, size), B),
+            pltpu.VMEM((length, size), B),
+            pltpu.VMEM((length, size), B),
+            pltpu.VMEM((length, 3 * size), B),
+            pltpu.VMEM((length, size), F),
+            pltpu.VMEM((length, size), F),
+            pltpu.VMEM((2, CHUNK, hidden), B),
+            pltpu.VMEM((2, CHUNK, hidden), F),
+            pltpu.SemaphoreType.DMA((27,)),
+            pltpu.SemaphoreType.DMA((27,)),
+            pltpu.SemaphoreType.DMA((3,)),
+            pltpu.SemaphoreType.DMA((2, 2)),
+            pltpu.SemaphoreType.DMA((2, 5)),
+            pltpu.SemaphoreType.DMA((2, 2)),
+            pltpu.SemaphoreType.DMA((5,)),
+        ],
+        compiler_params=pltpu.CompilerParams(
+            collective_id=0, has_side_effects=True, vmem_limit_bytes=67043328
+        ),
+        cost_estimate=pl.CostEstimate(flops=40 * 10**9, bytes_accessed=10**8, transcendentals=10**7),
+        name="gather",
+    )(mine, theirs, own_x, own_g, vectors, up_here, offsets, *tables, seg_col, seg_row)
+    mixed_sum = mixed_sum.reshape(heads, 3, size)
+    w_qkv, w_dense = weights[0, :, : 3 * size], weights[0, :, 3 * size :]
+    w_up, w_down = weights[1], weights[2]
+    last[0] = attn_send
+
+    near, far = slice(0, width // 2), slice(width // 2, width)
+
+    def partial(pairs, columns, kind):
+        return jnp.concatenate([dot(left[:, columns], right, ((0,), (0,)), kind) for left, right in pairs], axis=1)
+
+    def scattered(*pairs):
+        (send,) = done(partial(pairs, far, B))
+        pairs = [after(*pair) for pair in pairs]
+        (keep,) = done(partial(pairs, near, F))
+        return scatter(send, keep)
+
+    attn_near, attn_far = scatter(attn_send, attn_keep)
+
+    tile = 512
+    tiles = (count // tile,)
+    down_near, down_far = scattered((g_pair, activation))
+    pre_grad, up_bias_sum = done(
+        *call(
+            pre_kernel,
+            tiles,
+            [tiled(tile, width), shared(width, hidden), tiled(tile, hidden)],
+            [tiled(tile, hidden), shared(1, hidden)],
+            [shape((count, hidden), B), shape((1, hidden), F)],
+            2 * count * width * hidden,
+            20 * count * hidden,
+            name="pre_grad",
+        )(g_pair, w_down, slope)
+    )
+    blend, norm_sums = done(
+        *call(
+            lambda *refs: blend_kernel(step, *refs),
+            tiles,
+            [
+                tiled(tile, 3 * size),
+                tiled(tile, hidden),
+                shared(width, 3 * size),
+                shared(width, hidden),
+                tiled(tile, width),
+                shared(6, width),
+            ],
+            [tiled(tile, width), shared(4, width)],
+            [shape((count, width), B), shape((4, width), F)],
+            2 * count * width * (hidden + 3 * size),
+            20 * count * hidden,
+            prefetch=1,
+            name="blend",
+        )(order_table, mixed_grad, pre_grad, w_qkv, w_up, x_pair, vectors)
+    )
+    blend_held, blend_sent = total_rows(blend)
+    context, activation, w_dense, w_down = after(context, activation, w_dense, w_down)
+    (branch,) = done(
+        call(
+            branch_kernel,
+            tiles,
+            [tiled(tile, size), tiled(tile, hidden), shared(width, size), shared(width, hidden)],
+            tiled(tile, width),
+            shape((count, width), B),
+            2 * count * width * (hidden + size),
+            20 * count * hidden,
+            name="branch",
+        )(context, activation, w_dense, w_down)
+    )
+    branch_held, branch_sent = total_rows(branch)
+    up_near, up_far = scattered((mlp_in, pre_grad))
+
+    quarter = length // 4
+    x_rows, g_rows = own_rows(own_x, 0), own_rows(own_g, 0)
+    rows_out = shape((quarter, width), B)
+    row_spec = tiled(quarter // 2, width)
+
+    def finished(kernel, name, *operands):
+        specs = [row_spec if a.shape[0] == quarter else shared(*a.shape) for a in operands]
+        return call(
+            lambda *refs: kernel(step, *refs), (2,), specs, row_spec, rows_out, 10 * quarter * width, 10 * quarter * width,
+            prefetch=1, name=name,
+        )(place_table, *operands)
+
+    input_grad = share_rows(finished(finish_grad, "finish_grad", blend_held, blend_sent, x_rows, g_rows))
+    block_out = share_rows(finished(finish_out, "finish_out", branch_held, branch_sent, x_rows, vectors))
+
+    def by_half(near, far):
+        return jnp.where(half == 0, jnp.stack([near, far]), jnp.stack([far, near]))
+
+    attn_shard = by_half(attn_near, attn_far)
+    qkv_shard = attn_shard[:, :, : 3 * size].transpose(1, 0, 2)
+    dense_shard = attn_shard[:, :, 3 * size :].transpose(0, 2, 1)
+    up_shard = jnp.where(half == 0, jnp.concatenate([up_near, up_far], 1), jnp.concatenate([up_far, up_near], 1))
+    down_shard = by_half(down_near, down_far).transpose(0, 2, 1)
+
+    bias_sum = jnp.sum(own_g.astype(F), axis=0)
+
+    def slotted(array):
+        zero = jnp.zeros_like(array)
+        return join(array, zero, half, 0)
+
+    small = [norm_sums.reshape(-1), bias_sum, slotted(up_bias_sum[0]), slotted(mixed_sum).reshape(-1)]
+    sizes = [s.shape[0] for s in small]
+    flat = jnp.concatenate(small)
+    for bit in [1 << k for k in range(groups.bit_length() - 1)]:
+        flat = flat + swap(flat, bit)
+    ends = [sum(sizes[: i + 1]) for i in range(len(sizes))]
+    norms = flat[: ends[0]]
+    for bit in [1 << k for k in range(ways.bit_length() - 1)]:
+        norms = norms + cross(norms, bit)
+    norms = norms.reshape(4, width)
+    bias_grad = flat[ends[0] : ends[1]]
+    up_bias_grad = flat[ends[1] : ends[2]]
+    mixed_bias = flat[ends[2] :].reshape(2 * heads, 3, size)
+    qv_grad = jnp.stack([mixed_bias[:, 0], mixed_bias[:, 2]], axis=1)
+    key_bias_grad = mixed_bias[:, 1, :ROT]
+
+    return (
+        block_out[None],
+        input_grad[None],
+        norms[0],
+        norms[1],
+        norms[2],
+        norms[3],
+        qkv_shard.reshape(qkv_weight.shape),
+        qv_grad,
+        key_bias_grad,
+        dense_shard.reshape(dense_weight.shape),
+        bias_grad,
+        up_shard,
+        up_bias_grad,
+        down_shard.reshape(down_weight.shape),
+        bias_grad,
+    )
+
+
 def solution(mesh):
     placed = (
         P("dp", None, None),
@@ -378,7 +1163,10 @@
     )
 
     def whole(*arrays):
-        return body(*arrays, groups=mesh.shape["dp"], ways=mesh.shape["tensor"])
+        groups, ways = mesh.shape["dp"], mesh.shape["tensor"]
+        part = arrays[0].shape[2] // groups
+        chosen = body_narrow if part % 128 or groups != 8 else body
+        return chosen(*arrays, groups=groups, ways=ways)
 
     return jax.shard_map(
         whole,

time: 859 us -> 674 us (0.78)
  Pallas kernels: 21.8 us -> 264 us
  waiting for transfers between devices: 330 us -> 184 us
  matrix products: 168 us -> 32.3 us
  local copies, waits for them, and re-layouts: 163 us -> 72 us
  other arithmetic: 115 us -> 74.9 us
    pallas_call x2 -> x6, Pallas kernels: 21.8 us -> 264 us  [the longest x1 196 us: body(): pl.pallas_call(functools.partial(gather_kernel, groups), in_specs=[hbm] *...]
    dot_general x16 -> x4, matrix products: 168 us -> 32.3 us  [dot(): lax.dot_general(left, right, (dims, ((), ())), preferred_element_type=F)]
    ppermute x36 -> x15, waiting for transfers between devices: 266 us -> 133 us  [swap(): return lax.ppermute(array, 'dp', [(i, i ^ bit) for i in range(groups)])]
    unnamed x278 -> x88, local copies, waits for them, and re-layouts: 88.3 us -> 15.6 us
    select_n x14 -> x2, other arithmetic: 40.4 us -> 0.01 us  [join(): return jnp.where(index == 0, pair, turned)]
    unnamed x27 -> x2, other arithmetic: 17.1 us -> 0.01 us
    select_n x0 -> x7, other arithmetic: none -> 16.5 us  [the longest x2 7.41 us: share_rows(): jnp.where(core == 0, quad, jnp.concatenate([quad[1:], quad[:1]], axis=0))]
    rev x2 -> x0, local copies, waits for them, and re-layouts: 15.7 us -> none  [total_rows(): jnp.flip(sent.reshape(rows, groups // 2, 2, part), axis=2)]
  transfers between devices with their start and end apart: 50 -> 25, of which waited for: 21 -> 10; matrix products, arithmetic and copies ran while one was open for 34% -> 21% of each run, Pallas kernels for 1% -> 1%
where the time goes in v2:
time: 674 us; the launch traced here: 665 us
  Pallas kernels  264 us (39%)
  waiting for transfers between devices  184 us (27%)
  other arithmetic  74.9 us (11%)
  local copies, waits for them, and re-layouts  72 us (11%)
  starting transfers between devices  35.8 us (5%)
  matrix products  32.3 us (5%)
    pallas_call x1, Pallas kernels, body(): pl.pallas_call(functools.partial(gather_kernel, groups), in_specs=[hbm] *...  196 us
    ppermute x15, waiting for transfers between devices, swap(): return lax.ppermute(array, 'dp', [(i, i ^ bit) for i in range(groups)])  133 us
    ppermute x10, waiting for transfers between devices, cross(): return lax.ppermute(array, 'tensor', [(i, i ^ bit) for i in range(ways)])  51.1 us
    dot_general x4, matrix products, dot(): lax.dot_general(left, right, (dims, ((), ())), preferred_element_type=F)  32.3 us
    pallas_call x1, Pallas kernels, body(): call(lambda *refs: blend_kernel(step, *refs), tiles, [tiled(tile, 3 * siz...  28.3 us
    ppermute x15, starting transfers between devices, swap(): return lax.ppermute(array, 'dp', [(i, i ^ bit) for i in range(groups)])  27.8 us
    dynamic_slice x9, local copies, waits for them, and re-layouts, pick(): return lax.dynamic_slice_in_dim(array, index * rows, rows, axis)  18.2 us
    pallas_call x1, Pallas kernels, body(): call(branch_kernel, tiles, [tiled(tile, size), tiled(tile, hidden), share...  16.1 us
  transfers between devices with their start and end apart: 25, of which 10 were waited for; matrix products, arithmetic and copies ran while one was open for 21% of the time, Pallas kernels for 1%

profile of v2, /device:TPU:0, one launch (start us, length us, event | category | flops | bytes accessed | tf_op | source)
XLA Modules:
  0.0 664.5 jit_solution(7758451040056368201)
XLA Ops:
  26.5 3.4 convert_reduce_fusion
  44.9 195.9 %gather.7 = (bf16[3,2048,1024]{2,1,0:T(8,128)(2,1)}, bf16[1024,2048]{1,0:T(8,128)(2,1)}, bf16[1024,2048]{1,0:T(8,128)(2,1)}, bf16[2048,2048]{1,0:T(8,128)(2,1)},...) custom-call(bf16[3,256,1024]{2,1,0:T(8,128)(2,1)} %pad_maximum_fusio, ...), custom_call_target="tpu_custom_call" | custom-call | flops 40000000000 | bytes 100000000 | tf_op jit(solution)/shard_map/gather/pallas_call | solution.py:957
  243.1 6.0 slice_bitcast_fusion
  249.1 3.8 slice_bitcast_fusion.2.refs_3_
  252.9 14.4 %pre_grad.1 = (bf16[2048,1024]{1,0:T(8,128)(2,1)}, f32[1,1024]{1,0:T(1,128)}) custom-call(bf16[2048,2048]{1,0:T(8,128)(2,1)} %get-tuple-element.59.g_ref, bf16[2048,1024]{1,0:T(8,128)(2,1)} %get-tuple-element.51.w_ref.down_ref, f32[2048,1024]{1,0:T(8,128)} %get-tuple-element.43.slope_ref), custom_call_target="tpu_custom_call" | custom-call | flops 8589934592 | bytes 41943040 | tf_op jit(solution)/shard_map/pre_grad/pallas_call | solution.py:1032
  267.2 28.3 %blend.1 = (bf16[2048,2048]{1,0:T(8,128)(2,1)}, f32[4,2048]{1,0:T(4,128)}) custom-call(s32[8]{0:T(128)} %broadcast_xor_fusion.refs_0_, bf16[2048,768]{1,0:T(8,128)(2,1)} %get-tuple-element.41.refs_1_, bf16[2048,1024]{1,0:T(8,128)(2,1)} %get-tuple-element.58.refs_2_, bf16[2048,768]{1,0:T(8,128)(2,1)} %slice_bitcast_fusion.2.refs_3_, ...), custom_call_target="tpu_custom_call" | custom-call | flops 15032385536 | bytes 41943040 | tf_op jit(solution)/shard_map/blend/pallas_call | solution.py:1044
  295.6 8.0 %fusion.22 = bf16[1024,1024]{1,0:T(8,128)(2,1)} fusion(bf16[2048,1024]{1,0:T(8,128)(2,1)S(1)} %copy-done.35, bf16[2048,2048]{1,0:T(8,128)(2,1)} %get-tuple-element.59.g_ref), kind=kOutput, calls=%fused_computation.59 | convolution fusion | flops 4296015872 | bytes 10485760 | tf_op jit(solution)/shard_map/dot_general | solution.py:19
  303.5 16.1 %branch.1 = bf16[2048,2048]{1,0:T(8,128)(2,1)} custom-call(bf16[2048,256]{1,0:T(8,128)(2,1)} %get-tuple-element.48.ctx_ref, bf16[2048,1024]{1,0:T(8,128)(2,1)} %get-tuple-element.60.act_ref, bf16[2048,256]{1,0:T(8,128)(2,1)} %slice_bitcast_fusion.6.dense_ref, bf16[2048,1024]{1,0:T(8,128)(2,1)} %get-tuple-element.51.w_ref.down_ref), custom_call_target="tpu_custom_call" | custom-call | flops 10737418240 | bytes 41943040 | tf_op jit(solution)/shard_map/branch/pallas_call | solution.py:1066
  319.7 5.1 constant_dynamic-slice_fusion.2
  324.7 3.5 collective-permute-start.1
  333.5 9.6 %fusion.19 = bf16[1024,1024]{1,0:T(8,128)(2,1)} fusion(bf16[2048,1024]{1,0:T(8,128)(2,1)} %get-tuple-element.58.refs_2_, bf16[2048,2048]{1,0:T(8,128)(2,1)} %get-tuple-element.57), kind=kOutput, calls=%fused_computation.58 | convolution fusion | flops 4296015872 | bytes 10485760 | tf_op jit(solution)/shard_map/dot_general | solution.py:19
  345.2 8.5 %fusion.6 = f32[1024,1024]{1,0:T(8,128)} fusion(bf16[2048,1024]{1,0:T(8,128)(2,1)S(1)} %copy-done.37, bf16[2048,2048]{1,0:T(8,128)(2,1)} %get-tuple-element.57), kind=kOutput, calls=%fused_computation.22 | convolution fusion | flops 4294967296 | bytes 12582912 | tf_op jit(solution)/shard_map/dot_general | solution.py:19
  353.8 5.5 collective-permute-start.13
  359.3 6.3 fusion.2
  366.3 7.1 %add_convert_fusion.1 = (bf16[2,256,2048]{2,1,0:T(8,128)(2,1)}, f32[2,256,2048]{2,1,0:T(8,128)S(1)}) fusion(bf16[2,512,2048]{2,1,0:T(8,128)(2,1)} %collective-permute-done.1, s32[]{:T(128)S(6)} %select_n.182, bf16[2,1024,2048]{2,1,0:T(8,128)(2,1)} %bitcast.98, s32[]{:T(128)S(6)} %dynamic_slice.92, s32[]{:T(128)S(6)} %select_n.177, s32[]{:T(128)S(6)} %dynamic_slice.88), kind=kLoop, calls=%fused_computation.29 | loop fusion | flops 7340032 | bytes 14680080 | tf_op jit(solution)/shard_map/convert_element_type | solution.py:910
  376.6 45.6 %collective-permute-done.15 = f32[8192]{0:T(1024)S(1)} collective-permute-done((f32[8192]{0:T(1024)S(1)}, f32[8192]{0:T(1024)S(1)}, u32[]{:S(2)}, u32[]{:S(2)}) %collective-permute-start.15) | collective-permute-done | bytes 32800 | tf_op jit(solution)/shard_map/ppermute | solution.py:858
  424.3 7.2 %add_convert_fusion = (bf16[2,256,2048]{2,1,0:T(8,128)(2,1)}, f32[2,256,2048]{2,1,0:T(8,128)S(1)}) fusion(bf16[2,512,2048]{2,1,0:T(8,128)(2,1)} %collective-permute-done.6, s32[]{:T(128)S(6)} %select_n.182, bf16[2,1024,2048]{2,1,0:T(8,128)(2,1)} %bitcast.95, s32[]{:T(128)S(6)} %dynamic_slice.92, s32[]{:T(128)S(6)} %select_n.177, s32[]{:T(128)S(6)} %dynamic_slice.88), kind=kLoop, calls=%fused_computation.27 | loop fusion | flops 7340032 | bytes 14680080 | tf_op jit(solution)/shard_map/convert_element_type | solution.py:910
  432.5 4.4 collective-permute-done.16
  445.8 3.8 fusion.25
  452.5 27.9 %collective-permute-done.22 = bf16[1024,1024]{1,0:T(8,128)(2,1)S(1)} collective-permute-done((bf16[1024,1024]{1,0:T(8,128)(2,1)}, bf16[1024,1024]{1,0:T(8,128)(2,1)S(1)}, u32[]{:S(2)}, u32[]{:S(2)}) %collective-permute-start.22) | collective-permute-done | bytes 2097184 | tf_op jit(solution)/shard_map/ppermute | solution.py:855
  484.9 5.9 collective-permute-start.8
  490.8 18.6 %collective-permute-done.3.refs_2_ = bf16[256,2048]{1,0:T(8,128)(2,1)S(1)} collective-permute-done((bf16[256,2048]{1,0:T(8,128)(2,1)S(1)}, bf16[256,2048]{1,0:T(8,128)(2,1)S(1)}, u32[]{:S(2)}, u32[]{:S(2)}) %collective-permute-start.3) | collective-permute-done | bytes 1048608 | tf_op jit(solution)/shard_map/ppermute | solution.py:855
  510.4 3.9 finish_out.1
  514.6 17.9 %collective-permute-done.17 = bf16[512,1024]{1,0:T(8,128)(2,1)S(1)} collective-permute-done((bf16[512,1024]{1,0:T(8,128)(2,1)}, bf16[512,1024]{1,0:T(8,128)(2,1)S(1)}, u32[]{:S(2)}, u32[]{:S(2)}) %collective-permute-start.17) | collective-permute-done | bytes 1048608 | tf_op jit(solution)/shard_map/ppermute | solution.py:855
  536.0 40.9 %collective-permute-done.23 = bf16[512,1024]{1,0:T(8,128)(2,1)S(1)} collective-permute-done((bf16[512,1024]{1,0:T(8,128)(2,1)}, bf16[512,1024]{1,0:T(8,128)(2,1)S(1)}, u32[]{:S(2)}, u32[]{:S(2)}) %collective-permute-start.23) | collective-permute-done | bytes 1048608 | tf_op jit(solution)/shard_map/ppermute | solution.py:855
  578.4 5.0 finish_grad.1
  592.1 7.4 %collective-permute-done.18 = f32[256,1024]{1,0:T(8,128)} collective-permute-done((f32[256,1024]{1,0:T(8,128)}, f32[256,1024]{1,0:T(8,128)}, u32[]{:S(2)}, u32[]{:S(2)}) %collective-permute-start.18) | collective-permute-done | bytes 1048608 | tf_op jit(solution)/shard_map/ppermute | solution.py:855
  601.4 5.5 collective-permute-done.9
  613.4 3.7 copy.49
  628.1 15.1 %collective-permute-done.21 = f32[256,1024]{1,0:T(8,128)} collective-permute-done((f32[256,1024]{1,0:T(8,128)}, f32[256,1024]{1,0:T(8,128)}, u32[]{:S(2)}, u32[]{:S(2)}) %collective-permute-start.21) | collective-permute-done | bytes 1048608 | tf_op jit(solution)/shard_map/ppermute | solution.py:855
  656.1 3.7 maximum_select_fusion
  659.8 3.7 maximum_select_fusion.1
  (212 shorter events, 121.3 us)
Async XLA Ops:
  0.6 42.3 %collective-permute-start = (s32[1024]{0:T(1024)}, s32[1024]{0:T(1024)S(1)}, u32[]{:S(2)}, u32[]{:S(2)}) collective-permute-start(s32[1024]{0:T(1024)} %bitcast.125), channel_id=1, source_target_pairs={{0,8},{4,12},{8,0},{12,4},{16,24},{20,28},{24,16},{28,20},{1,9},{5... | collective-permute-start | bytes 12296 | tf_op jit(solution)/shard_map/ppermute | solution.py:855
  267.2 28.3 %copy-start.35 = (bf16[2048,1024]{1,0:T(8,128)(2,1)S(1)}, bf16[2048,1024]{1,0:T(8,128)(2,1)}, u32[]{:S(2)}) copy-start(bf16[2048,1024]{1,0:T(8,128)(2,1)} %get-tuple-element.60.act_ref) | copy-start | bytes 12582916
  324.7 41.6 %collective-permute-start.1 = (bf16[2,512,2048]{2,1,0:T(8,128)(2,1)}, bf16[2,512,2048]{2,1,0:T(8,128)(2,1)}, u32[]{:S(2)}, u32[]{:S(2)}) collective-permute-start(bf16[2,512,2048]{2,1,0:T(8,128)(2,1)} %constant_dynamic-slice_fusion.2), channel_id=1, source_target_pairs={{0,1},{1,0},{2,3},{3,2},{4,5},{5,4},{6,7},{7,6},{8,9},{9,8},{10,11... | collective-permute-start | bytes 12582920 | tf_op jit(solution)/shard_map/ppermute | solution.py:858
  330.6 93.7 %collective-permute-start.6 = (bf16[2,512,2048]{2,1,0:T(8,128)(2,1)}, bf16[2,512,2048]{2,1,0:T(8,128)(2,1)}, u32[]{:S(2)}, u32[]{:S(2)}) collective-permute-start(bf16[2,512,2048]{2,1,0:T(8,128)(2,1)} %constant_dynamic-slice_fusion), channel_id=1, source_target_pairs={{0,1},{1,0},{2,3},{3,2},{4,5},{5,4},{6,7},{7,6},{8,9},{9,8},{10,11... | collective-permute-start | bytes 12582920 | tf_op jit(solution)/shard_map/ppermute | solution.py:858
  331.8 13.3 %collective-permute-start.11 = (f32[13824]{0:T(1024)S(1)}, f32[13824]{0:T(1024)S(1)}, u32[]{:S(2)}, u32[]{:S(2)}) collective-permute-start(f32[13824]{0:T(1024)S(1)} %pad_maximum_fusion.6), channel_id=1, source_target_pairs={{0,4},{4,0},{8,12},{12,8},{16,20},{20,16},{24,28},{28,24},{1,5},{5... | collective-permute-start | bytes 165896 | tf_op jit(solution)/shard_map/ppermute | solution.py:855
  343.1 97.5 %collective-permute-start.19 = (bf16[1024,1024]{1,0:T(8,128)(2,1)}, bf16[1024,1024]{1,0:T(8,128)(2,1)S(1)}, u32[]{:S(2)}, u32[]{:S(2)}) collective-permute-start(bf16[1024,1024]{1,0:T(8,128)(2,1)} %fusion.19), channel_id=1, source_target_pairs={{0,4},{4,0},{8,12},{12,8},{16,20},{20,16},{24,28},{28,24},{1,5},{5... | collective-permute-start | bytes 6291464 | tf_op jit(solution)/shard_map/ppermute | solution.py:855
  343.4 93.4 %collective-permute-start.16 = (bf16[1024,1024]{1,0:T(8,128)(2,1)}, bf16[1024,1024]{1,0:T(8,128)(2,1)}, u32[]{:S(2)}, u32[]{:S(2)}) collective-permute-start(bf16[1024,1024]{1,0:T(8,128)(2,1)} %get-tuple-element.55), channel_id=1, source_target_pairs={{0,4},{4,0},{8,12},{12,8},{16,20},{20,16},{24,28},{28,24},{1,5},{5... | collective-permute-start | bytes 6291464 | tf_op jit(solution)/shard_map/ppermute | solution.py:855
  345.1 14.1 %slice-start = ((s8[8388608]{0:T(1024)(128)(4,1)}), s8[4194304]{0:T(1024)(128)(4,1)S(1)}, s32[]{:S(2)}) async-start(s8[8388608]{0:T(1024)(128)(4,1)} %bitcast.130), calls=%async_computation | async-start | bytes 8388608
  345.1 14.1 %slice-start.1 = ((s8[8388608]{0:T(1024)(128)(4,1)}), s8[4194304]{0:T(1024)(128)(4,1)S(1)}, s32[]{:S(2)}) async-start(s8[8388608]{0:T(1024)(128)(4,1)} %bitcast.130), calls=%async_computation.1 | async-start | bytes 8388608
  345.2 8.6 %collective-permute-start.12 = (f32[13824]{0:T(1024)S(1)}, f32[13824]{0:T(1024)S(1)}, u32[]{:S(2)}, u32[]{:S(2)}) collective-permute-start(f32[13824]{0:T(1024)S(1)} %fusion.34), channel_id=1, source_target_pairs={{0,8},{4,12},{8,0},{12,4},{16,24},{20,28},{24,16},{28,20},{1,9},{5... | collective-permute-start | bytes 165896 | tf_op jit(solution)/shard_map/ppermute | solution.py:855
  353.8 11.8 %collective-permute-start.13 = (f32[13824]{0:T(1024)S(1)}, f32[13824]{0:T(1024)S(1)}, u32[]{:S(2)}, u32[]{:S(2)}) collective-permute-start(f32[13824]{0:T(1024)S(1)} %add.175), channel_id=1, source_target_pairs={{0,16},{4,20},{8,24},{12,28},{16,0},{20,4},{24,8},{28,12},{1,17},{... | collective-permute-start | bytes 165896 | tf_op jit(solution)/shard_map/ppermute | solution.py:855
  366.2 297.3 %copy-start.21 = (f32[2048]{0:T(1024)}, f32[2048]{0:T(1024)S(1)}, u32[]{:S(2)}) copy-start(f32[2048]{0:T(1024)S(1)} %get-tuple-element.174) | copy-start | bytes 24580
  366.2 8.8 %collective-permute-start.14 = (f32[8192]{0:T(1024)S(1)}, f32[8192]{0:T(1024)S(1)}, u32[]{:S(2)}, u32[]{:S(2)}) collective-permute-start(f32[8192]{0:T(1024)S(1)} %slice.193), channel_id=1, source_target_pairs={{0,1},{1,0},{2,3},{3,2},{4,5},{5,4},{6,7},{7,6},{8,9},{9,8},{10,11... | collective-permute-start | bytes 98312 | tf_op jit(solution)/shard_map/ppermute | solution.py:858
  373.3 72.5 %collective-permute-start.2 = (bf16[2,256,2048]{2,1,0:T(8,128)(2,1)}, bf16[2,256,2048]{2,1,0:T(8,128)(2,1)}, u32[]{:S(2)}, u32[]{:S(2)}) collective-permute-start(bf16[2,256,2048]{2,1,0:T(8,128)(2,1)} %get-tuple-element.93), channel_id=1, source_target_pairs={{0,2},{1,3},{2,0},{3,1},{4,6},{5,7},{6,4},{7,5},{8,10},{9,11},{10,... | collective-permute-start | bytes 6291464 | tf_op jit(solution)/shard_map/ppermute | solution.py:858
  375.0 47.3 %collective-permute-start.15 = (f32[8192]{0:T(1024)S(1)}, f32[8192]{0:T(1024)S(1)}, u32[]{:S(2)}, u32[]{:S(2)}) collective-permute-start(f32[8192]{0:T(1024)S(1)} %slice_add_fusion.7), channel_id=1, source_target_pairs={{0,2},{1,3},{2,0},{3,1},{4,6},{5,7},{6,4},{7,5},{8,10},{9,11},{10,... | collective-permute-start | bytes 98312 | tf_op jit(solution)/shard_map/ppermute | solution.py:858
  422.3 58.2 %collective-permute-start.22 = (bf16[1024,1024]{1,0:T(8,128)(2,1)}, bf16[1024,1024]{1,0:T(8,128)(2,1)S(1)}, u32[]{:S(2)}, u32[]{:S(2)}) collective-permute-start(bf16[1024,1024]{1,0:T(8,128)(2,1)} %fusion.22), channel_id=1, source_target_pairs={{0,4},{4,0},{8,12},{12,8},{16,20},{20,16},{24,28},{28,24},{1,5},{5... | collective-permute-start | bytes 6291464 | tf_op jit(solution)/shard_map/ppermute | solution.py:855
  431.5 51.3 %collective-permute-start.7 = (bf16[2,256,2048]{2,1,0:T(8,128)(2,1)}, bf16[2,256,2048]{2,1,0:T(8,128)(2,1)S(1)}, u32[]{:S(2)}, u32[]{:S(2)}) collective-permute-start(bf16[2,256,2048]{2,1,0:T(8,128)(2,1)} %get-tuple-element.91), channel_id=1, source_target_pairs={{0,2},{1,3},{2,0},{3,1},{4,6},{5,7},{6,4},{7,5},{8,10},{9,11},{10,... | collective-permute-start | bytes 6291464 | tf_op jit(solution)/shard_map/ppermute | solution.py:858
  440.6 91.9 %collective-permute-start.17 = (bf16[512,1024]{1,0:T(8,128)(2,1)}, bf16[512,1024]{1,0:T(8,128)(2,1)S(1)}, u32[]{:S(2)}, u32[]{:S(2)}) collective-permute-start(bf16[512,1024]{1,0:T(8,128)(2,1)} %split.73), channel_id=1, source_target_pairs={{0,16},{4,20},{8,24},{12,28},{16,0},{20,4},{24,8},{28,12},{1,17},{... | collective-permute-start | bytes 3145736 | tf_op jit(solution)/shard_map/ppermute | solution.py:855
  443.2 143.8 %collective-permute-start.20 = (bf16[512,1024]{1,0:T(8,128)(2,1)}, bf16[512,1024]{1,0:T(8,128)(2,1)}, u32[]{:S(2)}, u32[]{:S(2)}) collective-permute-start(bf16[512,1024]{1,0:T(8,128)(2,1)} %split.72), channel_id=1, source_target_pairs={{0,16},{4,20},{8,24},{12,28},{16,0},{20,4},{24,8},{28,12},{1,17},{... | collective-permute-start | bytes 3145736 | tf_op jit(solution)/shard_map/ppermute | solution.py:855
  445.8 34.6 %copy-start.7 = (f32[1024,1024]{1,0:T(8,128)S(1)}, f32[1024,1024]{1,0:T(8,128)}, u32[]{:S(2)}) copy-start(f32[1024,1024]{1,0:T(8,128)} %fusion.2) | copy-start | bytes 12582916
  449.6 59.8 %collective-permute-start.3 = (bf16[256,2048]{1,0:T(8,128)(2,1)S(1)}, bf16[256,2048]{1,0:T(8,128)(2,1)S(1)}, u32[]{:S(2)}, u32[]{:S(2)}) collective-permute-start(bf16[256,2048]{1,0:T(8,128)(2,1)S(1)} %get-tuple-element.99), channel_id=1, source_target_pairs={{0,8},{4,12},{8,0},{12,4},{16,24},{20,28},{24,16},{28,20},{1,9},{5... | collective-permute-start | bytes 3145736 | tf_op jit(solution)/shard_map/ppermute | solution.py:855
  482.8 94.0 %collective-permute-start.23 = (bf16[512,1024]{1,0:T(8,128)(2,1)}, bf16[512,1024]{1,0:T(8,128)(2,1)S(1)}, u32[]{:S(2)}, u32[]{:S(2)}) collective-permute-start(bf16[512,1024]{1,0:T(8,128)(2,1)} %split.71), channel_id=1, source_target_pairs={{0,16},{4,20},{8,24},{12,28},{16,0},{20,4},{24,8},{28,12},{1,17},{... | collective-permute-start | bytes 3145736 | tf_op jit(solution)/shard_map/ppermute | solution.py:855
  484.9 93.5 %collective-permute-start.8 = (bf16[256,2048]{1,0:T(8,128)(2,1)S(1)}, bf16[256,2048]{1,0:T(8,128)(2,1)}, u32[]{:S(2)}, u32[]{:S(2)}) collective-permute-start(bf16[256,2048]{1,0:T(8,128)(2,1)S(1)} %get-tuple-element.97), channel_id=1, source_target_pairs={{0,8},{4,12},{8,0},{12,4},{16,24},{20,28},{24,16},{28,20},{1,9},{5... | collective-permute-start | bytes 3145736 | tf_op jit(solution)/shard_map/ppermute | solution.py:855
  514.3 69.5 %collective-permute-start.4 = (bf16[256,2048]{1,0:T(8,128)(2,1)}, bf16[256,2048]{1,0:T(8,128)(2,1)}, u32[]{:S(2)}, u32[]{:S(2)}) collective-permute-start(bf16[256,2048]{1,0:T(8,128)(2,1)} %finish_out.1), channel_id=1, source_target_pairs={{0,2},{1,3},{2,0},{3,1},{4,6},{5,7},{6,4},{7,5},{8,10},{9,11},{10,... | collective-permute-start | bytes 3145736 | tf_op jit(solution)/shard_map/ppermute | solution.py:858
  534.4 42.4 %copy-start.3 = (f32[1024,1024]{1,0:T(8,128)S(1)}, f32[1024,1024]{1,0:T(8,128)}, u32[]{:S(2)}) copy-start(f32[1024,1024]{1,0:T(8,128)} %copy-done.2) | copy-start | bytes 12582916
  536.0 63.5 %collective-permute-start.18 = (f32[256,1024]{1,0:T(8,128)}, f32[256,1024]{1,0:T(8,128)}, u32[]{:S(2)}, u32[]{:S(2)}) collective-permute-start(f32[256,1024]{1,0:T(8,128)} %get-tuple-element.114), channel_id=1, source_target_pairs={{0,8},{4,12},{8,0},{12,4},{16,24},{20,28},{24,16},{28,20},{1,9},{5... | collective-permute-start | bytes 3145736 | tf_op jit(solution)/shard_map/ppermute | solution.py:855
  578.4 43.5 %collective-permute-start.24 = (f32[256,1024]{1,0:T(8,128)}, f32[256,1024]{1,0:T(8,128)}, u32[]{:S(2)}, u32[]{:S(2)}) collective-permute-start(f32[256,1024]{1,0:T(8,128)} %get-tuple-element.110), channel_id=1, source_target_pairs={{0,8},{4,12},{8,0},{12,4},{16,24},{20,28},{24,16},{28,20},{1,9},{5... | collective-permute-start | bytes 3145736 | tf_op jit(solution)/shard_map/ppermute | solution.py:855
  583.4 23.5 %collective-permute-start.9 = (bf16[256,2048]{1,0:T(8,128)(2,1)}, bf16[256,2048]{1,0:T(8,128)(2,1)S(1)}, u32[]{:S(2)}, u32[]{:S(2)}) collective-permute-start(bf16[256,2048]{1,0:T(8,128)(2,1)} %finish_grad.1), channel_id=1, source_target_pairs={{0,2},{1,3},{2,0},{3,1},{4,6},{5,7},{6,4},{7,5},{8,10},{9,11},{10,... | collective-permute-start | bytes 3145736 | tf_op jit(solution)/shard_map/ppermute | solution.py:858
  586.9 59.6 %collective-permute-start.5 = (bf16[2,256,2048]{2,1,0:T(8,128)(2,1)}, bf16[2,256,2048]{2,1,0:T(8,128)(2,1)}, u32[]{:S(2)}, u32[]{:S(2)}) collective-permute-start(bf16[2,256,2048]{2,1,0:T(8,128)(2,1)} %get-tuple-element.118), channel_id=1, source_target_pairs={{0,1},{1,0},{2,3},{3,2},{4,5},{5,4},{6,7},{7,6},{8,9},{9,8},{10,11... | collective-permute-start | bytes 6291464 | tf_op jit(solution)/shard_map/ppermute | solution.py:858
  590.0 53.2 %collective-permute-start.21 = (f32[256,1024]{1,0:T(8,128)}, f32[256,1024]{1,0:T(8,128)}, u32[]{:S(2)}, u32[]{:S(2)}) collective-permute-start(f32[256,1024]{1,0:T(8,128)} %get-tuple-element.112), channel_id=1, source_target_pairs={{0,8},{4,12},{8,0},{12,4},{16,24},{20,28},{24,16},{28,20},{1,9},{5... | collective-permute-start | bytes 3145736 | tf_op jit(solution)/shard_map/ppermute | solution.py:855
  609.1 41.7 %collective-permute-start.10 = (bf16[2,256,2048]{2,1,0:T(8,128)(2,1)}, bf16[2,256,2048]{2,1,0:T(8,128)(2,1)}, u32[]{:S(2)}, u32[]{:S(2)}) collective-permute-start(bf16[2,256,2048]{2,1,0:T(8,128)(2,1)} %get-tuple-element.116), channel_id=1, source_target_pairs={{0,1},{1,0},{2,3},{3,2},{4,5},{5,4},{6,7},{7,6},{8,9},{9,8},{10,11... | collective-permute-start | bytes 6291464 | tf_op jit(solution)/shard_map/ppermute | solution.py:858
  625.2 18.1 %copy-start.10 = (f32[256,1024]{1,0:T(8,128)S(1)}, f32[256,1024]{1,0:T(8,128)}, u32[]{:S(2)}) copy-start(f32[256,1024]{1,0:T(8,128)} %get-tuple-element.111) | copy-start | bytes 3145732
  (33 other events, 151.0 us)

commit v3 on v2

--- a/solution.py
+++ b/solution.py
@@ -105,100 +105,12 @@
         sum_ref[0, :, number * size : (number + 1) * size] = jnp.sum(part.astype(F), axis=0, keepdims=True)
 
 
-def pre_kernel(g_ref, w_ref, slope_ref, out_ref, sum_ref):
-    grad = (dot(g_ref[...], w_ref[...], ((1,), (0,)), F) * slope_ref[...]).astype(B)
-    out_ref[...] = grad
-
-    @pl.when(pl.program_id(0) == 0)
-    def _():
-        sum_ref[...] = jnp.zeros_like(sum_ref)
-
-    sum_ref[...] += jnp.sum(grad.astype(F), axis=0, keepdims=True)
-
-
-def branch_kernel(ctx_ref, act_ref, dense_ref, down_ref, out_ref):
-    width = out_ref.shape[1]
-    for low in range(0, width, 512):
-        here = slice(low, low + 512)
-        out_ref[:, here] = (
-            dot(ctx_ref[...], dense_ref[here, :], ((1,), (1,)), F)
-            + dot(act_ref[...], down_ref[here, :], ((1,), (1,)), F)
-        ).astype(B)
-
-
-def blend_kernel(part, order_ref, mixed_ref, pre_ref, qkv_ref, up_ref, x_ref, vec_ref, out_ref, sum_ref):
-    @pl.when(pl.program_id(0) == 0)
-    def _():
-        sum_ref[...] = jnp.zeros_like(sum_ref)
-
-    rows = x_ref[...].astype(F)
-    mean = jnp.mean(rows, axis=1, keepdims=True)
-    center = rows - mean
-    inverse = lax.rsqrt(jnp.mean(center * center, axis=1, keepdims=True) + 1e-05)
-    for place in range(x_ref.shape[1] // part):
-        here = slice(place * part, (place + 1) * part)
-        there = pl.ds(pl.multiple_of(order_ref[place] * part, part), part)
-        attn_grad = dot(mixed_ref[...], qkv_ref[here, :], ((1,), (1,)), F)
-        mlp_grad = dot(pre_ref[...], up_ref[here, :], ((1,), (1,)), F)
-        normed = (x_ref[:, here].astype(F) - mean) * inverse
-        out_ref[:, here] = (attn_grad * vec_ref[0:1, there] + mlp_grad * vec_ref[2:3, there]).astype(B)
-        sum_ref[0:1, there] += jnp.sum(attn_grad * normed, axis=0, keepdims=True)
-        sum_ref[1:2, there] += jnp.sum(attn_grad, axis=0, keepdims=True)
-        sum_ref[2:3, there] += jnp.sum(mlp_grad * normed, axis=0, keepdims=True)
-        sum_ref[3:4, there] += jnp.sum(mlp_grad, axis=0, keepdims=True)
-
-
-def finish_out(part, place_ref, held_ref, sent_ref, x_ref, vec_ref, out_ref):
-    for block in range(x_ref.shape[1] // part):
-        here = slice(block * part, (block + 1) * part)
-        place, other = place_ref[0, block], place_ref[1, block]
-        mine = held_ref[:, pl.ds(pl.multiple_of(place * part, part), part)]
-        theirs = sent_ref[:, pl.ds(pl.multiple_of(other * part, part), part)].astype(F)
-        bias = vec_ref[4:5, here] + vec_ref[5:6, here]
-        out_ref[:, here] = (x_ref[:, here].astype(F) + (mine + theirs) + bias).astype(B)
-
-
-def finish_grad(part, place_ref, held_ref, sent_ref, x_ref, g_ref, out_ref):
-    rows = x_ref[...].astype(F)
-    mean = jnp.mean(rows, axis=1, keepdims=True)
-    center = rows - mean
-    inverse = lax.rsqrt(jnp.mean(center * center, axis=1, keepdims=True) + 1e-05)
-    blends = []
-    for block in range(x_ref.shape[1] // part):
-        place, other = place_ref[0, block], place_ref[1, block]
-        mine = held_ref[:, pl.ds(pl.multiple_of(place * part, part), part)]
-        theirs = sent_ref[:, pl.ds(pl.multiple_of(other * part, part), part)].astype(F)
-        blends.append(mine + theirs)
-    blend = jnp.concatenate(blends, axis=1)
-    normed = center * inverse
-    inner = blend - jnp.mean(blend, axis=1, keepdims=True) - normed * jnp.mean(blend * normed, axis=1, keepdims=True)
-    out_ref[...] = (g_ref[...].astype(F) + inner * inverse).astype(B)
-
-
 def per_seq(rows, columns):
     return pl.BlockSpec((1, rows, columns), lambda seq, *_: (seq, 0, 0))
 
 
 def shared(rows, columns):
     return pl.BlockSpec((rows, columns), lambda *_: (0, 0))
-
-
-def tiled(rows, columns):
-    return pl.BlockSpec((rows, columns), lambda tile, *_: (tile, 0))
-
-
-def call(kernel, grid, in_specs, out_specs, out_shape, flops, moved, prefetch=0, aliases=None, scratch=(), name=None):
-    return pl.pallas_call(
-        kernel,
-        grid_spec=pltpu.PrefetchScalarGridSpec(
-            num_scalar_prefetch=prefetch, grid=grid, in_specs=in_specs, out_specs=out_specs, scratch_shapes=list(scratch)
-        ),
-        out_shape=out_shape,
-        input_output_aliases=aliases or {},
-        cost_estimate=pl.CostEstimate(flops=flops, bytes_accessed=moved, transcendentals=0),
-        compiler_params=pltpu.CompilerParams(vmem_limit_bytes=56 * 1024 * 1024),
-        name=name,
-    )
 
 
 MESH = pl.DeviceIdType.MESH
@@ -266,6 +178,7 @@
     send_out,
     keep_out,
     sum_ref,
+    bias_ref,
     w,
     raw_x,
     raw_g,
@@ -359,6 +272,8 @@
             here = pl.ds(pl.multiple_of(tile * CHUNK, CHUNK), CHUNK)
             both = pl.ds(pl.multiple_of(seq * length + tile * CHUNK, CHUNK), CHUNK)
             mean, inverse = stats(raw_x[slot].astype(F))
+            if seq == 0:
+                bias_ref[...] += jnp.sum(raw_g[slot].astype(F), axis=0, keepdims=True)
             for position, mask in enumerate(order):
                 to = slice(position * part, (position + 1) * part)
                 there = pl.ds(pl.multiple_of(flip(me, mask) * part, part), part)
@@ -486,6 +401,7 @@
     own = [pltpu.make_async_copy(mine_ref.at[group], w.at[group, rows(0)], own_sem.at[group]) for group in range(3)]
     for copy in own:
         copy.start()
+    bias_ref[...] = jnp.zeros_like(bias_ref)
     first_out = normalise(0, x_ref, g_ref)
     for copy in first_out:
         copy.start()
@@ -570,6 +486,537 @@
         copy.wait_send()
 
 
+def scatter_kernel(
+    groups,
+    attn_send,
+    attn_keep,
+    weights,
+    x_rel,
+    g_rel,
+    mlp_in,
+    mixed_grad,
+    context,
+    activation,
+    slope,
+    x_ref,
+    g_ref,
+    vec_ref,
+    mixed_sum,
+    bias_sum,
+    block_out,
+    input_grad,
+    near_out,
+    far_out,
+    y_recv,
+    z_recv,
+    c_recv,
+    x_recv,
+    e_recv,
+    small_out,
+    w,
+    act_v,
+    pre_v,
+    tile_v,
+    col_v,
+    slope_t,
+    mix_t,
+    ctx_v,
+    keep_v,
+    y_send,
+    z_send,
+    y_stage,
+    c_send,
+    c_stage,
+    r_stage,
+    x_send,
+    hold_v,
+    mean_v,
+    inverse_v,
+    e_send,
+    sum_v,
+    small_v,
+    small_recv,
+    load_sem,
+    tile_sem,
+    ys_sem,
+    yr_sem,
+    zs_sem,
+    zr_sem,
+    ps_sem,
+    pr_sem,
+    cs_sem,
+    cr_sem,
+    xs_sem,
+    xr_sem,
+    es_sem,
+    er_sem,
+    fs_sem,
+    fr_sem,
+    ss_sem,
+    sr_sem,
+    out_sem,
+):
+    length, width = x_ref.shape
+    part = width // groups
+    size = context.shape[1]
+    hidden = activation.shape[1]
+    quarter = length // 4
+    me, place = lax.axis_index("dp"), lax.axis_index("tensor")
+    core, side, half = lax.rem(place, 2), lax.div(place, 2), bit_of(me, PAIR)
+    pair_to, side_to, core_to = flip(me, PAIR), flip(place, 2), flip(place, 1)
+    spread, order = block_order(groups)
+    z_to, y_to = [flip(me, bit) for bit in spread]
+    greet([("dp", pair_to), ("dp", z_to), ("dp", y_to), ("tensor", side_to), ("tensor", core_to)])
+
+    def remote(source, target, send, recv, axis, index):
+        return pltpu.make_async_remote_copy(
+            src_ref=source, dst_ref=target, send_sem=send, recv_sem=recv, device_id={axis: index}, device_id_type=MESH
+        )
+
+    def span(position, count=1):
+        return pl.ds(position * part, count * part)
+
+    def step(index, amount):
+        return pl.ds(pl.multiple_of(index * amount, amount), amount)
+
+    def y_copy(group, position):
+        source = attn_send if group == 0 else y_send
+        here = step(position, part) if not isinstance(position, int) else span(position)
+        return remote(
+            source.at[here], y_recv.at[group, here], ys_sem.at[group, position], yr_sem.at[group, position], "dp", y_to
+        )
+
+    def z_copy(group, position):
+        return remote(
+            z_send.at[slot_of[group], span(position)],
+            z_recv.at[group, span(position)],
+            zs_sem.at[group, position],
+            zr_sem.at[group, position],
+            "dp",
+            z_to,
+        )
+
+    slot_of = (0, 0, 1)
+
+    def p_copy(group):
+        return remote(
+            keep_v.at[slot_of[group], span(1)], far_out.at[group], ps_sem.at[group], pr_sem.at[group], "dp", pair_to
+        )
+
+    def near_copy(group):
+        return pltpu.make_async_copy(keep_v.at[slot_of[group], span(0)], near_out.at[group], out_sem.at[group])
+
+    def staged(source):
+        copy = pltpu.make_async_copy(source, y_stage, load_sem.at[6])
+        copy.start()
+        copy.wait()
+
+    def y_far(group):
+        for position in (3, 2):
+            y_copy(group, position).wait_recv()
+            staged(y_recv.at[group, span(position)])
+            total = keep_v[slot_of[group], span(position)] + y_stage[...].astype(F)
+            if group == 1:
+                z_copy(0, position - 2).wait_send()
+            z_send[slot_of[group], span(position - 2)] = total.astype(B)
+            z_copy(group, position - 2).start()
+
+    def y_near(group):
+        for position in (1, 0):
+            y_copy(group, position).wait_recv()
+            staged(y_recv.at[group, span(position)])
+            keep_v[slot_of[group], span(position)] += y_stage[...].astype(F)
+
+    def z_last(group, position):
+        z_copy(group, position).wait_recv()
+        staged(z_recv.at[group, span(position)])
+        keep_v[slot_of[group], span(position)] += y_stage[...].astype(F)
+        if position == 1:
+            p_copy(group).start()
+        else:
+            near_copy(group).start()
+
+    loads = [
+        pltpu.make_async_copy(weights.at[2], w.at[2], load_sem.at[0]),
+        pltpu.make_async_copy(weights.at[0], w.at[0], load_sem.at[1]),
+        pltpu.make_async_copy(weights.at[1], w.at[1], load_sem.at[2]),
+        pltpu.make_async_copy(activation, act_v, load_sem.at[3]),
+        pltpu.make_async_copy(context, ctx_v, load_sem.at[4]),
+        pltpu.make_async_copy(attn_keep, keep_v.at[0], load_sem.at[5]),
+    ]
+    for copy in loads:
+        copy.start()
+    for position in (3, 2, 1, 0):
+        y_copy(0, position).start()
+
+    small_v[...] = jnp.zeros_like(small_v)
+
+    def pre_load(tile, slot):
+        here = step(tile, CHUNK)
+        return (
+            pltpu.make_async_copy(g_rel.at[here], tile_v.at[step(slot, CHUNK)], tile_sem.at[0, slot]),
+            pltpu.make_async_copy(slope.at[here], slope_t.at[slot], tile_sem.at[1, slot]),
+        )
+
+    for copy in pre_load(0, 0):
+        copy.start()
+    sum_v[...] = jnp.zeros_like(sum_v)
+    loads[0].wait()
+
+    def pre_tile(tile, carry):
+        slot = lax.rem(tile, 2)
+
+        @pl.when(tile + 1 < 2 * length // CHUNK)
+        def _():
+            for copy in pre_load(tile + 1, 1 - slot):
+                copy.start()
+
+        for copy in pre_load(tile, slot):
+            copy.wait()
+        grad = (dot(tile_v[step(slot, CHUNK)], w[2], ((1,), (0,)), F) * slope_t[slot]).astype(B)
+        pre_v[step(tile, CHUNK)] = grad
+        sum_v[...] += jnp.sum(grad.astype(F), axis=0, keepdims=True)
+        return carry
+
+    lax.fori_loop(0, 2 * length // CHUNK, pre_tile, 0)
+
+    tall = 2 * quarter
+    blocks = width // CHUNK
+
+    def c_copy(which, seq, block):
+        here = step(block, CHUNK)
+        return remote(
+            c_send.at[:, here],
+            c_recv.at[which, seq, :, here],
+            cs_sem.at[which, seq, block],
+            cr_sem.at[which, seq, block],
+            "tensor",
+            core_to,
+        )
+
+    def x_copy(which, seq):
+        return remote(
+            x_send.at[which, seq], x_recv.at[which, seq], xs_sem.at[which, seq], xr_sem.at[which, seq], "tensor", side_to
+        )
+
+    def e_copy(which):
+        return remote(e_send.at[which], e_recv.at[which], es_sem.at[which], er_sem.at[which], "dp", pair_to)
+
+    def send_tile(which, seq, begin, block_of):
+        start = pl.multiple_of(seq * length + (1 - core) * tall, tall)
+        begin(start)
+
+        def one(block, carry):
+            value = block_of(start, block)
+            if (which, seq) != (0, 1):
+                before = (0, 1) if seq == 0 and which == 0 else ((0, 0) if seq == 1 else (1, 1))
+                c_copy(*before, block).wait_send()
+            c_send[:, step(block, CHUNK)] = value.astype(B)
+            c_copy(which, seq, block).start()
+            return carry
+
+        lax.fori_loop(0, blocks, one, 0)
+
+    def c_load(which, seq, block, slot):
+        return pltpu.make_async_copy(c_recv.at[which, seq, :, step(block, CHUNK)], c_stage.at[slot], tile_sem.at[2, slot])
+
+    def keep_tile(which, seq, begin, block_of):
+        start = pl.multiple_of(seq * length + core * tall, tall)
+        begin(start)
+        c_copy(which, seq, 0).wait_recv()
+        c_load(which, seq, 0, 0).start()
+
+        def one(block, carry):
+            slot = lax.rem(block, 2)
+            value = block_of(start, block)
+
+            @pl.when(block + 1 < blocks)
+            def _():
+                c_copy(which, seq, block + 1).wait_recv()
+                c_load(which, seq, block + 1, 1 - slot).start()
+
+            c_load(which, seq, block, slot).wait()
+            r_stage[...] = value + c_stage[slot].astype(F)
+            here = step(block, CHUNK)
+            hold_v[which, seq, :, here] = r_stage[step(side, quarter)]
+            x_send[which, seq, :, here] = r_stage[step(1 - side, quarter)].astype(B)
+            return carry
+
+        lax.fori_loop(0, blocks, one, 0)
+        x_copy(which, seq).start()
+
+    def blend_begin(start):
+        copies = (
+            pltpu.make_async_copy(x_rel.at[pl.ds(start, tall)], tile_v, tile_sem.at[3, 0]),
+            pltpu.make_async_copy(mixed_grad.at[pl.ds(start, tall)], mix_t, tile_sem.at[3, 1]),
+        )
+        for copy in copies:
+            copy.start()
+        for copy in copies:
+            copy.wait()
+        for slot in range(2):
+            mean, inverse = stats(tile_v[span_rows(slot)].astype(F))
+            mean_v[span_rows(slot)] = jnp.broadcast_to(mean, (CHUNK, 128))
+            inverse_v[span_rows(slot)] = jnp.broadcast_to(inverse, (CHUNK, 128))
+
+    def span_rows(slot):
+        return pl.ds(slot * CHUNK, CHUNK)
+
+    def natural_block(position):
+        result = me
+        for level, bit in enumerate([PAIR] + spread):
+            flipped = lax.rem(lax.div(position, 1 << level), 2)
+            result = result + bit * (1 - 2 * bit_of(me, bit)) * flipped
+        return result
+
+    def blend_block(start, block):
+        here = step(block, CHUNK)
+        there = step(natural_block(block), part)
+        attn_grad = dot(mix_t[...], w[0, here, : 3 * size], ((1,), (1,)), F)
+        mlp_grad = dot(pre_v[pl.ds(start, tall)], w[1, here, :], ((1,), (1,)), F)
+        mean, inverse = mean_v[...], inverse_v[...]
+        mean = jnp.concatenate([mean] * (CHUNK // 128), axis=1)
+        inverse = jnp.concatenate([inverse] * (CHUNK // 128), axis=1)
+        normed = (tile_v[:, here].astype(F) - mean) * inverse
+        small_v[0:1, there] += jnp.sum(attn_grad * normed, axis=0, keepdims=True)
+        small_v[1:2, there] += jnp.sum(attn_grad, axis=0, keepdims=True)
+        small_v[2:3, there] += jnp.sum(mlp_grad * normed, axis=0, keepdims=True)
+        small_v[3:4, there] += jnp.sum(mlp_grad, axis=0, keepdims=True)
+        return attn_grad * vec_ref[0:1, there] + mlp_grad * vec_ref[2:3, there]
+
+    for copy in loads[1:3]:
+        copy.wait()
+    send_tile(0, 1, blend_begin, blend_block)
+    loads[5].wait()
+    y_far(0)
+    send_tile(0, 0, blend_begin, blend_block)
+    keep_tile(0, 1, blend_begin, blend_block)
+    keep_tile(0, 0, blend_begin, blend_block)
+
+    small_v[4:5] = bias_sum[...]
+    small_v[5:6, step(half, hidden)] = sum_v[...]
+    small_v[6:7, pl.ds(pl.multiple_of(half * (width // 2), width // 2), 3 * size)] = mixed_sum[...]
+    rounds = [("dp", flip(me, bit)) for bit in [PAIR] + spread] + [("tensor", side_to), ("tensor", core_to)]
+
+    def small_copy(number):
+        return remote(small_v, small_recv.at[number], ss_sem.at[number], sr_sem.at[number], *rounds[number])
+
+    def small_end(number):
+        small_copy(number).wait()
+        if number < 3:
+            small_v[...] += small_recv[number]
+        else:
+            small_v[0:4] += small_recv[number, 0:4]
+        if number + 1 < len(rounds):
+            small_copy(number + 1).start()
+
+    small_copy(0).start()
+
+    def product(columns, right, group, positions, sent, old=None):
+        count = len(positions)
+        base = positions[0]
+        sign = positions[1] - positions[0] if count > 1 else 1
+
+        def load(number, slot):
+            return pltpu.make_async_copy(
+                columns.at[:, step(base + sign * number, part)], col_v.at[slot], tile_sem.at[4, slot]
+            )
+
+        load(0, 0).start()
+
+        def one(number, carry):
+            slot = lax.rem(number, 2)
+
+            @pl.when(number + 1 < count)
+            def _():
+                load(number + 1, 1 - slot).start()
+
+            load(number, slot).wait()
+            value = dot(col_v[slot], right[...], ((0,), (0,)), F)
+            position = base + sign * number
+            if sent:
+                if old is not None:
+                    y_copy(old, position - groups // 2).wait_send()
+                y_send[step(position - groups // 2, part)] = value.astype(B)
+                y_copy(group, position - groups // 2).start()
+            else:
+                keep_v[slot_of[group], step(position, part)] = value
+            return carry
+
+        lax.fori_loop(0, count, one, 0)
+
+    loads[3].wait()
+    product(g_rel, act_v, 2, (7, 6, 5, 4), True)
+    small_end(0)
+    product(g_rel, act_v, 2, (3, 2, 1, 0), False)
+    y_near(0)
+    small_end(1)
+
+    loads[4].wait()
+
+    def branch_begin(start):
+        pass
+
+    def branch_block(start, block):
+        here, rows = step(block, CHUNK), pl.ds(start, tall)
+        return dot(ctx_v[rows], w[0, here, 3 * size :], ((1,), (1,)), F) + dot(
+            act_v[rows], w[2, here, :], ((1,), (1,)), F
+        )
+
+    def read_stage(source):
+        copy = pltpu.make_async_copy(source, tile_v.at[pl.ds(0, quarter)], load_sem.at[6])
+        copy.start()
+        copy.wait()
+
+    def e_start(which):
+        x_copy(which, 1).wait_recv()
+        read_stage(x_recv.at[which, 1])
+
+        def one(block, carry):
+            here = step(block, CHUNK)
+            e_send[which, :, here] = (hold_v[which, 1, :, here] + tile_v[0:quarter, here].astype(F)).astype(B)
+            return carry
+
+        lax.fori_loop(0, blocks, one, 0)
+        e_copy(which).start()
+
+    def gather_own(which):
+        x_copy(which, 0).wait_recv()
+        read_stage(x_recv.at[which, 0])
+
+        def one(block, carry):
+            here = step(block, CHUNK)
+            hold_v[which, 0, :, here] += tile_v[0:quarter, here].astype(F)
+            return carry
+
+        lax.fori_loop(0, blocks, one, 0)
+
+    def spot(c, s):
+        return pl.ds(pl.multiple_of(c * tall + s * quarter, quarter), quarter)
+
+    def position_of(block, shifted=False):
+        result = 0
+        for level, bit in enumerate([PAIR] + spread):
+            mine = bit_of(me, bit)
+            if shifted and bit == PAIR:
+                mine = 1 - mine
+            result = result + (1 << level) * ((1 - mine) if block & bit else mine)
+        return result
+
+    def finish(which, out_ref):
+        gather_own(which)
+        e_copy(which).wait_recv()
+        copies = [
+            pltpu.make_async_copy(e_recv.at[which], tile_v.at[pl.ds(0, quarter)], load_sem.at[6]),
+            pltpu.make_async_copy(x_ref.at[spot(core, side)], tile_v.at[pl.ds(quarter, quarter)], load_sem.at[7]),
+        ]
+        if which == 0:
+            copies.append(pltpu.make_async_copy(g_ref.at[spot(core, side)], x_send.at[0, 0], load_sem.at[8]))
+            x_copy(0, 0).wait_send()
+        for copy in copies:
+            copy.start()
+        for copy in copies:
+            copy.wait()
+        here = pl.ds(which * quarter, quarter)
+        if which == 0:
+            total_u, total_un = 0.0, 0.0
+            mean, inverse = stats(tile_v[quarter:].astype(F))
+            for block in range(groups):
+                mine = hold_v[0, 0, :, step(position_of(block), part)]
+                theirs = tile_v[0:quarter, step(position_of(block, True), part)].astype(F)
+                blend = mine + theirs
+                normed = (tile_v[quarter:, block * part : (block + 1) * part].astype(F) - mean) * inverse
+                hold_v[0, 1, :, block * part : (block + 1) * part] = blend
+                total_u = total_u + jnp.sum(blend, axis=1, keepdims=True)
+                total_un = total_un + jnp.sum(blend * normed, axis=1, keepdims=True)
+            mean_u, mean_un = total_u * (1.0 / width), total_un * (1.0 / width)
+            for block in range(groups):
+                at = slice(block * part, (block + 1) * part)
+                normed = (tile_v[quarter:, at].astype(F) - mean) * inverse
+                inner = (hold_v[0, 1, :, at] - mean_u - normed * mean_un) * inverse
+                c_send[here, at] = (x_send[0, 0, :, at].astype(F) + inner).astype(B)
+        else:
+            for block in range(groups):
+                at = slice(block * part, (block + 1) * part)
+                mine = hold_v[1, 0, :, step(position_of(block), part)]
+                theirs = tile_v[0:quarter, step(position_of(block, True), part)].astype(F)
+                bias = vec_ref[4:5, at] + vec_ref[5:6, at]
+                c_send[here, at] = (tile_v[quarter:, at].astype(F) + (mine + theirs) + bias).astype(B)
+        first = remote(
+            c_send.at[here], out_ref.at[spot(core, side)], fs_sem.at[which, 0], fr_sem.at[which, 0], "tensor", side_to
+        )
+        second = remote(
+            c_send.at[here], out_ref.at[spot(core, side)], fs_sem.at[which, 1], fr_sem.at[which, 1], "tensor", core_to
+        )
+        own = pltpu.make_async_copy(c_send.at[here], out_ref.at[spot(core, side)], out_sem.at[3 + which])
+        for copy in (first, second, own):
+            copy.start()
+        return first, second, own
+
+    def finish_end(which, out_ref, copies):
+        first, second, own = copies
+        first.wait_recv()
+        third = remote(
+            out_ref.at[spot(core, 1 - side)],
+            out_ref.at[spot(core, 1 - side)],
+            fs_sem.at[which, 2],
+            fr_sem.at[which, 2],
+            "tensor",
+            core_to,
+        )
+        third.start()
+        return [first.wait_send, second.wait, third.wait, own.wait]
+
+    send_tile(1, 1, branch_begin, branch_block)
+    e_start(0)
+    small_end(2)
+    send_tile(1, 0, branch_begin, branch_block)
+    keep_tile(1, 1, branch_begin, branch_block)
+    keep_tile(1, 0, branch_begin, branch_block)
+    small_end(3)
+    y_far(2)
+    product(mlp_in, pre_v, 1, (7, 6, 5, 4), True, old=2)
+    small_end(4)
+    small_out[...] = small_v[...]
+    z_last(0, 1)
+    z_last(0, 0)
+    y_near(2)
+    for block in range(blocks):
+        c_copy(1, 0, block).wait_send()
+    copies_grad = finish(0, input_grad)
+    e_start(1)
+    p_copy(0).wait_send()
+    near_copy(0).wait()
+    product(mlp_in, pre_v, 1, (3, 2, 1, 0), False)
+    z_last(2, 1)
+    y_far(1)
+    ends = finish_end(0, input_grad, copies_grad)
+    z_last(2, 0)
+    copies_out = finish(1, block_out)
+    y_near(1)
+    z_last(1, 1)
+    ends += finish_end(1, block_out, copies_out)
+    z_last(1, 0)
+    for end in ends:
+        end()
+    for group in range(3):
+        p_copy(group).wait_recv()
+        if group:
+            p_copy(group).wait_send()
+            near_copy(group).wait()
+        for position in range(2):
+            if group:
+                z_copy(group, position).wait_send()
+        for position in range(4):
+            if group != 2:
+                y_copy(group, position).wait_send()
+    for which in range(2):
+        e_copy(which).wait_send()
+        for seq in range(2):
+            if (which, seq) != (0, 0):
+                x_copy(which, seq).wait_send()
+
+
 def body_narrow(
     tokens,
     segment_ids,
@@ -839,80 +1286,22 @@
 ):
     length, width = tokens.shape[1:]
     heads, size = qkv_weight.shape[1] // 2, qkv_weight.shape[3]
-    assert heads == 1
+    assert heads == 1 and ways == 4
     part = width // groups
     hidden = up_weight.shape[1] // 2
     count = 2 * length
     me = lax.axis_index("dp")
     half = (me // PAIR) % 2
-    place = lax.axis_index("tensor")
-    core, side = place % 2, place // 2
-    spread = [bit for bit in (1 << k for k in reversed(range(groups.bit_length() - 1))) if bit != PAIR]
     shape = jax.ShapeDtypeStruct
-    last = [me]
 
     def swap(array, bit):
         return lax.ppermute(array, "dp", [(i, i ^ bit) for i in range(groups)])
 
-    def cross(array, bit):
-        return lax.ppermute(array, "tensor", [(i, i ^ bit) for i in range(ways)])
-
-    def pick(array, index, axis, number=2):
-        rows = array.shape[axis] // number
+    def pick(array, index, axis):
+        rows = array.shape[axis] // 2
         return lax.dynamic_slice_in_dim(array, index * rows, rows, axis)
 
-    def join(mine, theirs, index, axis):
-        pair = jnp.concatenate([mine, theirs], axis=axis)
-        turned = jnp.concatenate([theirs, mine], axis=axis)
-        return jnp.where(index == 0, pair, turned)
-
-    def after(*values):
-        held, _ = lax.optimization_barrier((values, last[0]))
-        return held
-
-    def done(*values):
-        values = lax.optimization_barrier(values)
-        last[0] = values
-        return values
-
-    order = [0, PAIR]
-    for bit in spread:
-        order = order + [mask | bit for mask in order]
-    inverse = [order.index(mask) for mask in range(groups)]
-    held_at = jnp.asarray(inverse, jnp.int32)[jnp.arange(groups) ^ me]
-    place_table = jnp.stack([held_at, held_at ^ 1])
-    order_table = jnp.asarray(order, jnp.int32) ^ me
     vectors = jnp.stack([attn_norm_gain, attn_norm_bias, mlp_norm_gain, mlp_norm_bias, dense_bias, down_bias])
-    step = part
-
-    def scatter(send, keep):
-        held = keep + swap(send, spread[-1]).astype(F)
-        for bit in reversed(spread[:-1]):
-            keep, send = jnp.split(held, 2, axis=0)
-            held = keep + swap(send.astype(B), bit).astype(F)
-        keep, send = jnp.split(held, 2, axis=0)
-        return keep, swap(send, PAIR)
-
-    def share_rows(rows):
-        pair = jnp.stack([rows, cross(rows, 2)])
-        quad = jnp.stack([pair, cross(pair, 1)])
-        quad = jnp.where(side == 0, quad, jnp.concatenate([quad[:, 1:], quad[:, :1]], axis=1))
-        quad = jnp.where(core == 0, quad, jnp.concatenate([quad[1:], quad[:1]], axis=0))
-        return quad.reshape(length, width)
-
-    def own_rows(array, axis):
-        return pick(pick(array, core, axis), side, axis)
-
-    def total_rows(partial):
-        partial = partial.reshape(2, length, width)
-        near = cross(pick(partial, 1 - core, 1), 1)
-        keep = pick(partial, core, 1)
-        far = (pick(keep, 1 - side, 1).astype(F) + pick(near, 1 - side, 1).astype(F)).astype(B)
-        far = cross(far, 2)
-        keep = pick(keep, side, 1).astype(F) + pick(near, side, 1).astype(F)
-        sent = swap((keep[1] + far[1].astype(F)).astype(B), PAIR)
-        return keep[0] + far[0].astype(F), sent
-
     own_x, own_g = tokens[0], out_grad[0]
 
     shards = [
@@ -954,10 +1343,11 @@
         attn_send,
         attn_keep,
         mixed_sum,
+        bias_sum,
     ) = pl.pallas_call(
         functools.partial(gather_kernel, groups),
         in_specs=[hbm] * 4 + [vmem] * 8,
-        out_specs=[hbm] * 12 + [vmem],
+        out_specs=[hbm] * 12 + [vmem] * 2,
         out_shape=[
             shape((3, width, columns), B),
             shape((length, width), B),
@@ -972,6 +1362,7 @@
             shape((half_width, columns), B),
             shape((half_width, columns), F),
             shape((1, 3 * size), F),
+            shape((1, width), F),
         ],
         scratch_shapes=[
             pltpu.VMEM((3, width, columns), B),
@@ -1007,119 +1398,103 @@
         cost_estimate=pl.CostEstimate(flops=40 * 10**9, bytes_accessed=10**8, transcendentals=10**7),
         name="gather",
     )(mine, theirs, own_x, own_g, vectors, up_here, offsets, *tables, seg_col, seg_row)
-    mixed_sum = mixed_sum.reshape(heads, 3, size)
-    w_qkv, w_dense = weights[0, :, : 3 * size], weights[0, :, 3 * size :]
-    w_up, w_down = weights[1], weights[2]
-    last[0] = attn_send
-
-    near, far = slice(0, width // 2), slice(width // 2, width)
-
-    def partial(pairs, columns, kind):
-        return jnp.concatenate([dot(left[:, columns], right, ((0,), (0,)), kind) for left, right in pairs], axis=1)
-
-    def scattered(*pairs):
-        (send,) = done(partial(pairs, far, B))
-        pairs = [after(*pair) for pair in pairs]
-        (keep,) = done(partial(pairs, near, F))
-        return scatter(send, keep)
-
-    attn_near, attn_far = scatter(attn_send, attn_keep)
-
-    tile = 512
-    tiles = (count // tile,)
-    down_near, down_far = scattered((g_pair, activation))
-    pre_grad, up_bias_sum = done(
-        *call(
-            pre_kernel,
-            tiles,
-            [tiled(tile, width), shared(width, hidden), tiled(tile, hidden)],
-            [tiled(tile, hidden), shared(1, hidden)],
-            [shape((count, hidden), B), shape((1, hidden), F)],
-            2 * count * width * hidden,
-            20 * count * hidden,
-            name="pre_grad",
-        )(g_pair, w_down, slope)
+    quarter = length // 4
+    tall, blocks = 2 * quarter, width // CHUNK
+    rows_third = shape((3, part, columns), F)
+    dma = pltpu.SemaphoreType.DMA
+    block_out, input_grad, near, far, _, _, _, _, _, small = pl.pallas_call(
+        functools.partial(scatter_kernel, groups),
+        in_specs=[hbm] * 12 + [vmem] * 3,
+        out_specs=[hbm] * 9 + [vmem],
+        out_shape=[
+            shape((length, width), B),
+            shape((length, width), B),
+            rows_third,
+            rows_third,
+            shape((3, half_width, columns), B),
+            shape((3, half_width // 2, columns), B),
+            shape((2, 2, tall, width), B),
+            shape((2, 2, quarter, width), B),
+            shape((2, quarter, width), B),
+            shape((8, width), F),
+        ],
+        scratch_shapes=[
+            pltpu.VMEM((3, width, columns), B),
+            pltpu.VMEM((count, hidden), B),
+            pltpu.VMEM((count, hidden), B),
+            pltpu.VMEM((tall, width), B),
+            pltpu.VMEM((2, count, part), B),
+            pltpu.VMEM((2, CHUNK, hidden), F),
+            pltpu.VMEM((tall, 3 * size), B),
+            pltpu.VMEM((count, size), B),
+            pltpu.VMEM((2, half_width, columns), F),
+            pltpu.VMEM((half_width, columns), B),
+            pltpu.VMEM((2, half_width // 2, columns), B),
+            pltpu.VMEM((part, columns), B),
+            pltpu.VMEM((tall, width), B),
+            pltpu.VMEM((2, tall, CHUNK), B),
+            pltpu.VMEM((tall, CHUNK), F),
+            pltpu.VMEM((2, 2, quarter, width), B),
+            pltpu.VMEM((2, 2, quarter, width), F),
+            pltpu.VMEM((tall, 128), F),
+            pltpu.VMEM((tall, 128), F),
+            pltpu.VMEM((2, quarter, width), B),
+            pltpu.VMEM((1, hidden), F),
+            pltpu.VMEM((8, width), F),
+            pltpu.VMEM((5, 8, width), F),
+            dma((9,)),
+            dma((5, 2)),
+            dma((3, 4)),
+            dma((3, 4)),
+            dma((3, 2)),
+            dma((3, 2)),
+            dma((3,)),
+            dma((3,)),
+            dma((2, 2, blocks)),
+            dma((2, 2, blocks)),
+            dma((2, 2)),
+            dma((2, 2)),
+            dma((2,)),
+            dma((2,)),
+            dma((2, 3)),
+            dma((2, 3)),
+            dma((5,)),
+            dma((5,)),
+            dma((5,)),
+        ],
+        compiler_params=pltpu.CompilerParams(
+            collective_id=1, has_side_effects=True, vmem_limit_bytes=67043328
+        ),
+        cost_estimate=pl.CostEstimate(flops=60 * 10**9, bytes_accessed=10**8, transcendentals=10**7),
+        name="scatter",
+    )(
+        attn_send,
+        attn_keep,
+        weights,
+        x_pair,
+        g_pair,
+        mlp_in,
+        mixed_grad,
+        context,
+        activation,
+        slope,
+        own_x,
+        own_g,
+        vectors,
+        mixed_sum,
+        bias_sum,
     )
-    blend, norm_sums = done(
-        *call(
-            lambda *refs: blend_kernel(step, *refs),
-            tiles,
-            [
-                tiled(tile, 3 * size),
-                tiled(tile, hidden),
-                shared(width, 3 * size),
-                shared(width, hidden),
-                tiled(tile, width),
-                shared(6, width),
-            ],
-            [tiled(tile, width), shared(4, width)],
-            [shape((count, width), B), shape((4, width), F)],
-            2 * count * width * (hidden + 3 * size),
-            20 * count * hidden,
-            prefetch=1,
-            name="blend",
-        )(order_table, mixed_grad, pre_grad, w_qkv, w_up, x_pair, vectors)
-    )
-    blend_held, blend_sent = total_rows(blend)
-    context, activation, w_dense, w_down = after(context, activation, w_dense, w_down)
-    (branch,) = done(
-        call(
-            branch_kernel,
-            tiles,
-            [tiled(tile, size), tiled(tile, hidden), shared(width, size), shared(width, hidden)],
-            tiled(tile, width),
-            shape((count, width), B),
-            2 * count * width * (hidden + size),
-            20 * count * hidden,
-            name="branch",
-        )(context, activation, w_dense, w_down)
-    )
-    branch_held, branch_sent = total_rows(branch)
-    up_near, up_far = scattered((mlp_in, pre_grad))
-
-    quarter = length // 4
-    x_rows, g_rows = own_rows(own_x, 0), own_rows(own_g, 0)
-    rows_out = shape((quarter, width), B)
-    row_spec = tiled(quarter // 2, width)
-
-    def finished(kernel, name, *operands):
-        specs = [row_spec if a.shape[0] == quarter else shared(*a.shape) for a in operands]
-        return call(
-            lambda *refs: kernel(step, *refs), (2,), specs, row_spec, rows_out, 10 * quarter * width, 10 * quarter * width,
-            prefetch=1, name=name,
-        )(place_table, *operands)
-
-    input_grad = share_rows(finished(finish_grad, "finish_grad", blend_held, blend_sent, x_rows, g_rows))
-    block_out = share_rows(finished(finish_out, "finish_out", branch_held, branch_sent, x_rows, vectors))
-
-    def by_half(near, far):
-        return jnp.where(half == 0, jnp.stack([near, far]), jnp.stack([far, near]))
-
-    attn_shard = by_half(attn_near, attn_far)
-    qkv_shard = attn_shard[:, :, : 3 * size].transpose(1, 0, 2)
-    dense_shard = attn_shard[:, :, 3 * size :].transpose(0, 2, 1)
-    up_shard = jnp.where(half == 0, jnp.concatenate([up_near, up_far], 1), jnp.concatenate([up_far, up_near], 1))
-    down_shard = by_half(down_near, down_far).transpose(0, 2, 1)
-
-    bias_sum = jnp.sum(own_g.astype(F), axis=0)
-
-    def slotted(array):
-        zero = jnp.zeros_like(array)
-        return join(array, zero, half, 0)
-
-    small = [norm_sums.reshape(-1), bias_sum, slotted(up_bias_sum[0]), slotted(mixed_sum).reshape(-1)]
-    sizes = [s.shape[0] for s in small]
-    flat = jnp.concatenate(small)
-    for bit in [1 << k for k in range(groups.bit_length() - 1)]:
-        flat = flat + swap(flat, bit)
-    ends = [sum(sizes[: i + 1]) for i in range(len(sizes))]
-    norms = flat[: ends[0]]
-    for bit in [1 << k for k in range(ways.bit_length() - 1)]:
-        norms = norms + cross(norms, bit)
-    norms = norms.reshape(4, width)
-    bias_grad = flat[ends[0] : ends[1]]
-    up_bias_grad = flat[ends[1] : ends[2]]
-    mixed_bias = flat[ends[2] :].reshape(2 * heads, 3, size)
+
+    def by_half(group, columns=slice(None)):
+        mine, theirs = near[group, :, columns], far[group, :, columns]
+        return jnp.where(half == 0, jnp.stack([mine, theirs]), jnp.stack([theirs, mine]))
+
+    qkv_shard = by_half(0, slice(0, 3 * size)).transpose(1, 0, 2)
+    dense_shard = by_half(0, slice(3 * size, None)).transpose(0, 2, 1)
+    up_shard = jnp.where(half == 0, jnp.concatenate([near[1], far[1]], 1), jnp.concatenate([far[1], near[1]], 1))
+    down_shard = by_half(2).transpose(0, 2, 1)
+    norms, bias_grad, up_bias_grad = small[0:4], small[4], small[5]
+    mixed_bias = small[6].reshape(2, width // 2)[:, : 3 * size].reshape(2, 3, size)
     qv_grad = jnp.stack([mixed_bias[:, 0], mixed_bias[:, 2]], axis=1)
     key_bias_grad = mixed_bias[:, 1, :ROT]
 

time: 674 us -> 549 us (0.81)
  the two profiles are of different devices: /device:TPU:0 before, /device:TPU:5 now
where the time goes in v3:
time: 549 us; the launch traced here: 539 us
  Pallas kernels  482 us (88%)
  local copies, waits for them, and re-layouts  35.9 us (7%)
  other arithmetic  18.7 us (3%)
    pallas_call x1, Pallas kernels, body(): pl.pallas_call(functools.partial(scatter_kernel, groups), in_specs=[hbm]...  282 us
    pallas_call x1, Pallas kernels, body(): pl.pallas_call(functools.partial(gather_kernel, groups), in_specs=[hbm] *...  200 us
    unnamed x37, local copies, waits for them, and re-layouts  13.9 us
  transfers between devices with their start and end apart: 1, of which 0 were waited for; matrix products, arithmetic and copies ran while one was open for 4% of the time, Pallas kernels for 0%

profile of v3, /device:TPU:5, one launch (start us, length us, event | category | flops | bytes accessed | tf_op | source)
XLA Modules:
  0.0 539.2 jit_solution(12956757968109587298)
XLA Ops:
  0.6 1.4 collective-permute-start
  2.9 1.1 convert_bitcast_fusion
  3.9 2.4 copy.37
  6.9 1.7 convert_element_type.14
  8.6 0.8 reshape.59
  9.4 1.7 convert_element_type.15
  11.1 0.9 constant_dynamic-slice_fusion.2
  12.2 1.2 copy.50
  13.4 2.2 constant_dynamic-slice_fusion.3
  15.6 2.0 fusion.5
  18.0 1.3 pad_maximum_fusion.1.theirs_ref
  19.3 1.3 pad_maximum_fusion.mine_ref
  20.7 1.6 maximum_maximum_fusion.2
  23.6 0.7 stack.68.vec_ref
  24.9 1.3 copy.44.col_ref
  26.2 199.7 %gather.1 = (bf16[3,2048,1024]{2,1,0:T(8,128)(2,1)}, bf16[1024,2048]{1,0:T(8,128)(2,1)}, bf16[1024,2048]{1,0:T(8,128)(2,1)}, bf16[2048,2048]{1,0:T(8,128)(2,1)},...) custom-call(bf16[3,256,1024]{2,1,0:T(8,128)(2,1)} %pad_maximum_fusio, ...), custom_call_target="tpu_custom_call" | custom-call | flops 40000000000 | bytes 100000000 | tf_op jit(solution)/shard_map/gather/pallas_call | solution.py:1347
  226.0 282.1 %scatter.1 = (bf16[1024,2048]{1,0:T(8,128)(2,1)}, bf16[1024,2048]{1,0:T(8,128)(2,1)}, f32[3,256,1024]{2,1,0:T(8,128)}, f32[3,256,1024]{2,1,0:T(8,128)}, bf16[3,1...) custom-call(bf16[1024,1024]{1,0:T(8,128)(2,1)} %get-tuple-element.32, ...), custom_call_target="tpu_custom_call" | custom-call | flops 60000002048 | bytes 100000000 | tf_op jit(solution)/shard_map/scatter/pallas_call | solution.py:1405
  508.1 2.1 fusion.11
  510.8 1.0 slice.83
  511.7 2.1 slice.76
  513.8 2.9 fusion.9
  516.7 0.9 slice.77
  517.6 1.4 fusion.10
  519.1 1.0 copy.48
  520.1 1.9 fusion
  522.0 1.8 copy.46
  523.8 2.1 fusion.1
  526.4 2.1 copy.47
  529.1 3.3 maximum_select_fusion
  533.0 2.1 copy.60
  535.1 1.6 copy-done
  536.7 2.0 copy.61
  (57 shorter events, 6.2 us)
Async XLA Ops:
  0.6 23.6 %collective-permute-start = (s32[1024]{0:T(1024)}, s32[1024]{0:T(1024)S(1)}, u32[]{:S(2)}, u32[]{:S(2)}) collective-permute-start(s32[1024]{0:T(1024)} %bitcast.79), channel_id=1, source_target_pairs={{0,8},{4,12},{8,0},{12,4},{16,24},{20,28},{24,16},{28,20},{1,9},{5... | collective-permute-start | bytes 12296 | tf_op jit(solution)/shard_map/ppermute | solution.py:1298
  13.4 4.2 copy-start.13
  20.6 2.3 copy-start.12
  20.6 2.9 copy-start.5
  20.6 2.9 copy-start.6
  20.6 2.9 copy-start.7
  20.6 2.9 copy-start.8
  20.6 2.9 copy-start.9
  20.7 2.9 copy-start.10
  20.7 3.6 copy-start.11
  510.2 22.2 %copy-start.4 = (f32[1,2048]{1,0:T(1,128)}, f32[1,2048]{1,0:T(1,128)S(1)}, u32[]{:S(2)}) copy-start(f32[1,2048]{1,0:T(1,128)S(1)} %get-tuple-element.92) | copy-start | bytes 24580
  513.8 2.9 copy-start.3
  526.4 2.7 copy-start.2
  529.1 3.9 copy-start.1
  533.0 3.7 copy-start
